TPU v7x, 512 devices: a whole 4x4x16 slice. The times are simulated.
512 devices in a mesh: req: 64 (over z, x), mp: 8 (over y, core).
Axes of the slice: x: 4, y: 4, z: 16, core: 2. Of those that a mesh axis runs over, the one named last changes fastest.
Arguments:
- queries: bfloat16 [16384, 2048], P('req', 'mp')
- keys: bfloat16 [16384, 1024], P('req', 'mp'), may hold values from -6 to 6
- values: bfloat16 [16384, 1024], P('req', 'mp'), may hold values from -6 to 6
- out_weight: bfloat16 [2048, 4608], P(None, 'mp'), may hold values from -0.125 to 0.125
- out_grad: bfloat16 [16384, 4608], P('req', 'mp'), may hold values from -6 to 6
- bank: float32 [16384, 2, 1024], P('req', None, 'mp'), may hold values from -6 to 6
- moment_one: float32 [16384, 2, 1024], P('req', None, 'mp')
- moment_two: float32 [16384, 2, 1024], P('req', None, 'mp'), as said below
- block_list: int32 [64, 32], replicated, may hold values from 0 to 127, as said below
- block_count: int32 [64], replicated, may hold values from 19 to 32, as said below
- token_count: int32 [64], P('req'), may hold values from 128 to 256, as said below
Outputs:
- attn_out: float32 [16384, 4608], P('req', 'mp')
- bank_next: float32 [16384, 2, 1024], P('req', None, 'mp')
- moment_next: float32 [16384, 2, 1024], P('req', None, 'mp')
- second_next: float32 [16384, 2, 1024], P('req', None, 'mp')
Inputs may be any that keep to these rules, and one draw needn't show every extreme that they name: `block_list`: the 32 blocks of one request have distinct owners (block b belongs to owner b // 2). `block_count`: some request uses all 32 entries. The live tokens of a request are its first token_count[r] rows; some request fills all 256. `moment_two`: positive.
All inputs are finite; a program needn't handle non-finite values.
Results may differ from a plain program's by a relative error of at most 0.035.
Values may be sent and summed in bfloat16 or wider, within the bound.
A program may use at most 64 MiB of HBM per device.

v0:
```python
import jax
import jax.numpy as jnp
from jax import lax
from jax.sharding import PartitionSpec as P

HD = 128
BLOCK = 128


softcap = 50.0
qscale = 1.0 / 12.0
beta_one = 0.9
beta_two = 0.999
learn_rate = 0.3
adam_eps = 1e-08
bias_one = 1.0 - 0.9**10
bias_two = 1.0 - 0.999**10
span_blocks = 4


def capped(raw):
    return softcap * jnp.tanh(raw / softcap)


def key_scores(query_four, key_three):
    raw = jnp.einsum("tkgd,skd->kgts", query_four, key_three, preferred_element_type=jnp.float32)
    return capped(raw * qscale)


def to_slots(per_block, holder, owners):
    flat = per_block.reshape(holder.shape[0], -1)
    placed = jnp.zeros((owners, flat.shape[1]), flat.dtype).at[holder].set(flat)
    return placed.reshape((owners,) + per_block.shape[1:])


def from_slots(select, received):
    flat = received.reshape(received.shape[0], -1)
    return lax.dot_general(select, flat, (((0,), (0,)), ((), ())), precision=lax.Precision.HIGHEST)


def local(
    queries,
    keys,
    values,
    out_weight,
    out_grad,
    bank,
    moment_one,
    moment_two,
    block_list,
    block_count,
    token_count,
):
    owners = lax.axis_size("req")
    mine_index = lax.axis_index("req")
    tokens = queries.shape[0]
    kv_local = keys.shape[1] // HD
    group = queries.shape[1] // keys.shape[1]
    blk_dev = bank.shape[0] // BLOCK
    most_blocks = block_list.shape[1]
    steps = most_blocks // span_blocks
    width = span_blocks * BLOCK
    slot_index = lax.broadcasted_iota(jnp.int32, block_list.shape, 1)
    listed = (slot_index < block_count[:, None]) & (block_list // blk_dev == mine_index)
    local_ids = lax.broadcasted_iota(jnp.int32, block_list.shape + (blk_dev,), 2)
    wanted = listed[:, :, None] & (block_list[:, :, None] % blk_dev == local_ids)
    select = jnp.sum(wanted.astype(jnp.float32), axis=1)
    own_blocks = bank.astype(jnp.bfloat16).reshape(blk_dev, -1)
    outgoing = jnp.dot(
        select.astype(jnp.bfloat16), own_blocks, preferred_element_type=jnp.float32
    ).astype(jnp.bfloat16)
    outgoing = outgoing.reshape(owners, BLOCK, 2, keys.shape[1])
    fetched = lax.all_to_all(outgoing, "req", split_axis=0, concat_axis=0, tiled=True)
    my_list = lax.dynamic_index_in_dim(block_list, mine_index, 0, keepdims=False)
    my_blocks = lax.dynamic_index_in_dim(block_count, mine_index, 0, keepdims=False)
    my_tokens = token_count[0]
    holder = my_list // blk_dev
    prefix = jnp.take(fetched, holder, axis=0)
    prefix_keys = prefix[:, :, 0, :].reshape(steps, width, kv_local, HD)
    prefix_values = prefix[:, :, 1, :].reshape(steps, width, kv_local, HD)
    query_four = queries.reshape(tokens, kv_local, group, HD)
    token_keys = keys.reshape(tokens, kv_local, HD)
    token_values = values.reshape(tokens, kv_local, HD)
    position = lax.broadcasted_iota(jnp.int32, (tokens, tokens), 0)
    causal = position >= lax.broadcasted_iota(jnp.int32, (tokens, tokens), 1)
    token_exp = jnp.where(causal, jnp.exp(key_scores(query_four, token_keys)), 0.0)

    def prefix_exp(index):
        key_three = lax.dynamic_index_in_dim(prefix_keys, index, 0, keepdims=False)
        capped_scores = key_scores(query_four, key_three)
        slot = index * span_blocks + lax.broadcasted_iota(jnp.int32, (width,), 0) // BLOCK
        return (jnp.where(slot < my_blocks, jnp.exp(capped_scores), 0.0), capped_scores)

    def add_total(index, running):
        return running + jnp.sum(prefix_exp(index)[0], axis=-1)

    denominator = lax.fori_loop(0, steps, add_total, jnp.sum(token_exp, axis=-1))
    token_weights = (token_exp / denominator[..., None]).astype(jnp.bfloat16)
    mixed = jnp.einsum(
        "kgts,skd->tkgd", token_weights, token_values, preferred_element_type=jnp.float32
    )

    def add_values(index, running):
        weights = (prefix_exp(index)[0] / denominator[..., None]).astype(jnp.bfloat16)
        value_three = lax.dynamic_index_in_dim(prefix_values, index, 0, keepdims=False)
        return running + jnp.einsum(
            "kgts,skd->tkgd", weights, value_three, preferred_element_type=jnp.float32
        )

    mixed = lax.fori_loop(0, steps, add_values, mixed)
    row_ok = lax.broadcasted_iota(jnp.int32, (tokens, 1), 0) < my_tokens
    heads_out = jnp.where(row_ok, mixed.reshape(tokens, -1), 0.0).astype(jnp.bfloat16)
    rows = out_weight
    attn_out = jnp.dot(
        lax.all_gather(heads_out, "mp", axis=1, tiled=True),
        rows,
        preferred_element_type=jnp.float32,
    )
    rows = out_weight
    head_grad = lax.psum_scatter(
        lax.dot_general(
            rows, out_grad, (((1,), (1,)), ((), ())), preferred_element_type=jnp.float32
        ),
        "mp",
        scatter_dimension=0,
        tiled=True,
    )
    grad_heads = jnp.where(row_ok.reshape(1, tokens), head_grad, 0.0).astype(jnp.bfloat16)
    grad_heads = grad_heads.reshape(kv_local, group, HD, tokens)
    delta = jnp.einsum(
        "kgdt,tkgd->kgt",
        grad_heads,
        heads_out.reshape(tokens, kv_local, group, HD),
        preferred_element_type=jnp.float32,
    )

    def value_from(exps):
        weights = (exps / denominator[..., None]).astype(jnp.bfloat16)
        return jnp.einsum("kgts,kgdt->skd", weights, grad_heads, preferred_element_type=jnp.float32)

    def key_from(exps, capped_scores, index):
        value_three = lax.dynamic_index_in_dim(prefix_values, index, 0, keepdims=False)
        dprob = jnp.einsum(
            "kgdt,skd->kgts", grad_heads, value_three, preferred_element_type=jnp.float32
        )
        prob = exps / denominator[..., None]
        dscore = (
            prob * (dprob - delta[..., None]) * (1.0 - (capped_scores / softcap) ** 2) * qscale
        ).astype(jnp.bfloat16)
        return jnp.einsum("kgts,tkgd->skd", dscore, query_four, preferred_element_type=jnp.float32)

    empty = jnp.zeros((steps, width, kv_local, HD), jnp.float32)

    def per_block(grads):
        return grads.reshape(most_blocks, BLOCK, kv_local * HD)

    def both_step(index, grads):
        exps, capped_scores = prefix_exp(index)
        key_part = lax.dynamic_update_index_in_dim(
            grads[0], key_from(exps, capped_scores, index), index, 0
        )
        value_part = lax.dynamic_update_index_in_dim(grads[1], value_from(exps), index, 0)
        return (key_part, value_part)

    key_grads, value_grads = lax.fori_loop(0, steps, both_step, (empty, empty))
    stacked = jnp.stack((per_block(key_grads), per_block(value_grads)), axis=2)
    returned = lax.all_to_all(
        to_slots(stacked, holder, owners), "req", split_axis=0, concat_axis=0, tiled=True
    )
    block_grad = from_slots(select, returned).reshape(bank.shape)
    moment_next = beta_one * moment_one + (1.0 - beta_one) * block_grad
    second_next = beta_two * moment_two + (1.0 - beta_two) * block_grad * block_grad
    bank_next = bank - learn_rate * (moment_next / bias_one) / (
        jnp.sqrt(second_next / bias_two) + adam_eps
    )
    return (attn_out, bank_next, moment_next, second_next)


def solution(mesh):
    return jax.shard_map(
        local,
        mesh=mesh,
        in_specs=(
            P("req", "mp"),
            P("req", "mp"),
            P("req", "mp"),
            P(None, "mp"),
            P("req", "mp"),
            P("req", None, "mp"),
            P("req", None, "mp"),
            P("req", None, "mp"),
            P(),
            P(),
            P("req"),
        ),
        out_specs=(
            P("req", "mp"),
            P("req", None, "mp"),
            P("req", None, "mp"),
            P("req", None, "mp"),
        ),
        check_vma=False,
    )
```

profile of v0, /device:TPU:24, one launch (start us, length us, event | category | flops | bytes accessed | tf_op | source)
XLA Modules:
  0.0 771.4 jit_solution(15892292482261457871)
XLA Ops:
  9.9 3.3 convolution_convert_fusion
  13.2 7.7 reshape.378
  20.9 5.3 copy.62
  26.2 19.0 %all-to-all-start = ((bf16[64,128,2,128]{3,1,2,0:T(8,128)(2,1)}), bf16[64,128,2,128]{3,1,2,0:T(8,128)(2,1)}, u32[]{:S(2)}, u32[]{:S(2)}) async-start(bf16[64,128,2,128]{3,1,2,0:T(8,128)(2,1)} %copy.62), calls=%async_computation | async-start | bytes 8388608 | tf_op jit(solution)/shard_map/all_to_all | solution.py:73
  45.3 2.4 fusion.123
  50.3 184.9 %all-to-all-done = bf16[64,128,2,128]{3,1,2,0:T(8,128)(2,1)} async-done(((bf16[64,128,2,128]{3,1,2,0:T(8,128)(2,1)}), bf16[64,128,2,128]{3,1,2,0:T(8,128)(2,1)}, u32[]{:S(2)}, u32[]{:S(2)}) %all-to-all-start) | async-done | bytes 4194336 | tf_op jit(solution)/shard_map/all_to_all | solution.py:73
  235.2 4.3 gather_fusion
  242.8 16.5 %while.47 = (s32[]{:T(128)}, f32[1,2,256]{2,1,0:T(2,128)S(1)}, s32[]{:T(128)}, bf16[8,512,1,128]{3,1,2,0:T(8,128)(2,1)}, bf16[256,1,2,128]{3,0,2,1:T(8,128)(2,1)S(1)}, /*index=5*/s32[]{:T(128)}, s32[]{:T(128)}) while((s32[]{:T(128)}, f32[1,2,256]{2,1,0:T(2,128)S(1)}, s32[]{:T(128)}, bf16[8,512,1,128]{3,1,2,0:T(8,128)(2,1)}, ...), condition=%wide.region_4.5_spmd, body=%wide.region_2.4_spmd.sunk | while | flops 68162560 | bytes 271969 | solution.py:97
  259.8 18.5 %while.48 = (s32[]{:T(128)}, f32[256,1,2,128]{0,3,2,1:T(8,128)S(1)}, bf16[8,512,1,128]{3,1,0,2:T(8,128)(2,1)}, s32[]{:T(128)}, bf16[8,512,1,128]{3,1,2,0:T(8,128...) while((s32[]{:T(128)}, ...), condition=%wide.region_6.7_spmd, body=%wide.region_5.6_spmd.sunk | while | flops 135599104 | bytes 921713 | solution.py:110
  280.1 53.7 %while.49 = (s32[]{:T(128)}, f32[8,512,1,128]{3,1,2,0:T(8,128)}, f32[8,512,1,128]{3,1,2,0:T(8,128)}, s32[]{:T(128)}, bf16[8,512,1,128]{3,1,2,0:T(8,128)(2,1)}, /...) while((s32[]{:T(128)}, f32[8,512,1,128]{3,1,2,0:T(8,128)}, ...), condition=%wide.region_9.10_spmd, body=%wide.region_8.9_spmd.sunk | while | flops 272372736 | bytes 4466313 | solution.py:165
  282.5 2.4 fusion.171
  289.2 2.3 fusion.171
  295.9 2.3 fusion.171
  333.7 8.3 %pad_maximum_fusion = f32[32,128,2,128]{3,2,1,0:T(2,128)} fusion(f32[32,128,1,128]{3,2,1,0:T(1,128)} %bitcast.326, f32[32,128,1,128]{3,2,1,0:T(1,128)} %bitcast.325), kind=kLoop, calls=%fused_computation.112 | loop fusion | flops 1048576 | bytes 8388608 | tf_op jit(solution)/shard_map/stack | solution.py:166
  342.0 6.4 reshape.407
  348.4 8.1 %scatter_custom_fusion = f32[64,32768]{1,0:T(8,128)} fusion(s32[32]{0:T(128)} %copy-done.8, f32[32,32768]{1,0:T(8,128)} %reshape.407, f32[]{:T(128)} %constant.424.clone.1), kind=kCustom, calls=%fused_computation.113 | custom fusion | bytes 8389120 | tf_op jit(solution)/shard_map/scatter | solution.py:32
  356.6 11.7 %reshape.386 = f32[64,128,2,128]{3,2,1,0:T(2,128)} reshape(f32[64,32768]{1,0:T(8,128)} %scatter_custom_fusion) | data formatting | bytes 16777216 | tf_op jit(solution)/shard_map/reshape | solution.py:33
  368.3 6.2 all-to-all-start.1
  375.5 33.6 %all-gather.2.cloned.1.call-done = bf16[256,2048]{1,0:T(8,128)(2,1)} async-done(((bf16[256,256]{1,0:T(8,128)(2,1)}), bf16[256,2048]{1,0:T(8,128)(2,1)}) %all-gather.2.cloned.1.call-update) | async-done | bytes 1048592 | tf_op jit(solution)/shard_map/all_gather | solution.py:115
  409.1 2.8 fusion.122
  411.9 331.8 %all-to-all-done.1 = f32[64,128,2,128]{3,2,1,0:T(2,128)} async-done(((f32[64,128,2,128]{3,2,1,0:T(2,128)}), f32[64,128,2,128]{3,2,1,0:T(2,128)}, u32[]{:S(2)}, u32[]{:S(2)}) %all-to-all-start.1) | async-done | bytes 8388640 | tf_op jit(solution)/shard_map/all_to_all | solution.py:167
  743.8 11.5 %reshape.387 = f32[64,32768]{1,0:T(8,128)} reshape(f32[64,128,2,128]{3,2,1,0:T(2,128)} %all-to-all-done.1) | data formatting | bytes 16777216 | tf_op jit(solution)/shard_map/reshape | solution.py:37
  755.3 6.4 fusion.124
  762.0 2.6 divide_subtract_fusion
  (123 shorter events, 92.5 us)
Async XLA Ops:
  7.2 38.1 %copy-start = (bf16[2048,576]{0,1:T(8,128)(2,1)S(1)}, bf16[2048,576]{0,1:T(8,128)(2,1)}, u32[]{:S(2)}) copy-start(bf16[2048,576]{0,1:T(8,128)(2,1)} %param.20) | copy-start | bytes 7077892
  26.2 19.1 %copy-start.9 = (bf16[256,576]{0,1:T(8,128)(2,1)S(1)}, bf16[256,576]{0,1:T(8,128)(2,1)}, u32[]{:S(2)}) copy-start(bf16[256,576]{0,1:T(8,128)(2,1)} %param.21) | copy-start | bytes 884740
  26.2 208.9 %all-to-all-start = ((bf16[64,128,2,128]{3,1,2,0:T(8,128)(2,1)}), bf16[64,128,2,128]{3,1,2,0:T(8,128)(2,1)}, u32[]{:S(2)}, u32[]{:S(2)}) async-start(bf16[64,128,2,128]{3,1,2,0:T(8,128)(2,1)} %copy.62), calls=%async_computation | async-start | bytes 8388608 | tf_op jit(solution)/shard_map/all_to_all | solution.py:73
  45.2 2.5 copy-start.7
  45.2 3.1 copy-start.6
  45.2 233.1 %reduce-scatter.2.cloned.1.call-start = ((), (), s32[]{:S(2)}) async-start(), calls=%async_computation.4 | async-start | bytes 2359296 | tf_op jit(solution)/shard_map/reduce_scatter | solution.py:120
  47.7 1.5 copy-start.5
  47.7 2.3 copy-start.10
  49.4 0.5 copy-start.8
  242.8 16.6 %copy-start.11 = (bf16[256,128]{1,0:T(8,128)(2,1)S(1)}, bf16[256,128]{1,0:T(8,128)(2,1)}, u32[]{:S(2)}) copy-start(bf16[256,128]{1,0:T(8,128)(2,1)} %param.19) | copy-start | bytes 196612
  278.3 1.8 copy-start.1
  368.3 6.3 copy-start.2
  368.3 375.5 %all-to-all-start.1 = ((f32[64,128,2,128]{3,2,1,0:T(2,128)}), f32[64,128,2,128]{3,2,1,0:T(2,128)}, u32[]{:S(2)}, u32[]{:S(2)}) async-start(f32[64,128,2,128]{3,2,1,0:T(2,128)} %reshape.386), calls=%async_computation.2 | async-start | bytes 16777216 | tf_op jit(solution)/shard_map/all_to_all | solution.py:167
  374.5 34.6 %all-gather.2.cloned.1.call-start = ((), (), s32[]{:S(2)}) async-start(), calls=%async_computation.3 | async-start | bytes 1179648 | tf_op jit(solution)/shard_map/all_gather | solution.py:115
  755.3 6.7 copy-start.3
  755.3 6.8 copy-start.4
Sparse Core Ops, SparseCore 0:
  48.9 39.5 reduce-scatter.1
  378.0 31.0 all-gather.1
where the time goes:
time: 774 us; the launch traced here: 771 us
  waiting for transfers between devices  550 us (71%)
  matrix products  83.6 us (11%)
  local copies, waits for them, and re-layouts  58.7 us (8%)
  other arithmetic  38 us (5%)
  starting transfers between devices  25.3 us (3%)
  between operations  15 us (2%)
    all_to_all x1, waiting for transfers between devices, local(): lax.all_to_all(to_slots(stacked, holder, owners), 'req', split_axis=0, co...  332 us
    all_to_all x1, waiting for transfers between devices, local(): lax.all_to_all(outgoing, 'req', split_axis=0, concat_axis=0, tiled=True)  185 us
    all_gather x1, waiting for transfers between devices, local(): lax.all_gather(heads_out, 'mp', axis=1, tiled=True)  33.6 us
    dot_general x17, matrix products, key_scores(): jnp.einsum('tkgd,skd->kgts', query_four, key_three, preferred_element_typ...  21 us
    lt x24, other arithmetic, prefix_exp(): slot < my_blocks  20 us
    all_to_all x1, starting transfers between devices, local(): lax.all_to_all(outgoing, 'req', split_axis=0, concat_axis=0, tiled=True)  19 us
    dot_general x8, matrix products, key_from(): jnp.einsum('kgts,tkgd->skd', dscore, query_four, preferred_element_type=j...  18.6 us
    dot_general x8, matrix products, value_from(): jnp.einsum('kgts,kgdt->skd', weights, grad_heads, preferred_element_type=...  15.8 us
  transfers between devices with their start and end apart: 4, of which 3 were waited for; matrix products, arithmetic and copies ran while one was open for 6% of the time, Pallas kernels for 0%

commit v1 on v0

v1 whole, which is shorter than its diff:
```python
import functools

import jax
import jax.numpy as jnp
from jax import lax
from jax.experimental import pallas as pl
from jax.experimental.pallas import tpu as pltpu
from jax.sharding import PartitionSpec as P

HD = 128
BLOCK = 128
KEY, VALUE = 0, 1
RIGHT, LEFT = 0, 1

softcap = 50.0
qscale = 1.0 / 12.0
beta_one = 0.9
beta_two = 0.999
learn_rate = 0.3
adam_eps = 1e-08
bias_one = 1.0 - 0.9**10
bias_two = 1.0 - 0.999**10

NN = (((1,), (0,)), ((), ()))
NT = (((1,), (1,)), ((), ()))
TN = (((0,), (0,)), ((), ()))


def dot(a, b, dims):
    return lax.dot_general(a, b, dims, preferred_element_type=jnp.float32)


def choose(flag, a, b):
    return lax.select(flag, a, b)


def step_kernel(
    sizes,
    table,
    token_count,
    own_ref,
    q_ref,
    k_ref,
    v_ref,
    w_ref,
    og_ref,
    attn_ref,
    grad_ref,
    slab,
    queries,
    heads_grad,
    scaled_grad,
    exps,
    slopes,
    numer,
    denom,
    hg_send,
    hg_recv,
    stat_send,
    stat_recv,
    rows,
    num_send,
    num_recv,
    heads,
    part,
    own_sum,
    ring_send,
    ring_recv,
    ag_send_sem,
    ag_recv_sem,
    q_send_sem,
    q_recv_sem,
    g_send_sem,
    g_recv_sem,
    h_send_sem,
    h_recv_sem,
    s_send_sem,
    s_recv_sem,
    n_send_sem,
    n_recv_sem,
    a_send_sem,
    a_recv_sem,
    rs_send_sem,
    rs_recv_sem,
):
    Z, X, M, lag = sizes
    H = Z // 2
    tokens = q_ref.shape[0]
    group = q_ref.shape[1] // HD
    req, m = lax.axis_index("req"), lax.axis_index("mp")
    z, x = req // X, req % X
    right = {"req": ((z + 1) % Z) * X + x}
    left = {"req": ((z + Z - 1) % Z) * X + x}
    toward = (right, left)

    def x_peer(i):
        return {"req": z * X + (x + i) % X}

    def m_peer(i):
        return {"mp": (m + i) % M}

    def remote(src, dst, send_sem, recv_sem, device):
        return pltpu.make_async_remote_copy(
            src_ref=src,
            dst_ref=dst,
            send_sem=send_sem,
            recv_sem=recv_sem,
            device_id=device,
            device_id_type=pl.DeviceIdType.MESH,
        )

    def gather_hop(way, kind, hop):
        lane = way
        if way == LEFT and kind == VALUE:
            lane = 1 - hop // H
        return remote(
            slab.at[way, hop - 1, kind],
            slab.at[lane, hop, kind],
            ag_send_sem.at[way, hop, kind],
            ag_recv_sem.at[way, hop, kind],
            toward[way],
        )

    def last_hop(way, kind):
        return H if way == kind else H - 1

    def q_copy(i):
        return remote(
            q_ref, queries.at[x], q_send_sem.at[i], q_recv_sem.at[i], x_peer(i)
        )

    def g_copy(i):
        return remote(
            heads_grad.at[x], heads_grad.at[x], g_send_sem.at[i], g_recv_sem.at[i], x_peer(i)
        )

    def h_copy(i):
        return remote(
            hg_send.at[i], hg_recv.at[i], h_send_sem.at[i], h_recv_sem.at[i], m_peer(i)
        )

    def s_copy(i):
        return remote(stat_send, stat_recv.at[i], s_send_sem.at[i], s_recv_sem.at[i], x_peer(i))

    def n_copy(i):
        return remote(
            num_send.at[(x + i) % X], num_recv.at[i], n_send_sem.at[i], n_recv_sem.at[i], x_peer(i)
        )

    def a_copy(i):
        return remote(heads.at[m], heads.at[m], a_send_sem.at[i], a_recv_sem.at[i], m_peer(i))

    def ring_hop(way, kind, dist):
        return remote(
            ring_send.at[way, dist, kind],
            ring_recv.at[way, dist - 1, kind],
            rs_send_sem.at[way, dist, kind],
            rs_recv_sem.at[way, dist, kind],
            toward[way],
        )

    barrier = pltpu.get_barrier_semaphore()
    partners = [right, left] + [x_peer(i) for i in range(1, X)] + [m_peer(i) for i in range(1, M)]
    for partner in partners:
        pl.semaphore_signal(
            barrier, inc=1, device_id=partner, device_id_type=pl.DeviceIdType.MESH
        )
    own = own_ref[...]
    slab[RIGHT, 0] = own
    slab[LEFT, 0] = own
    slab[LEFT, H] = own
    queries[x] = q_ref[...]
    pl.semaphore_wait(barrier, len(partners))

    for kind in (KEY, VALUE):
        for way in (RIGHT, LEFT):
            gather_hop(way, kind, 1).start()
    for i in range(1, X):
        q_copy(i).start()

    def share(i, carry):
        target = (m + i) % M
        band = pl.ds(pl.multiple_of(target * (group * HD), group * HD), group * HD)
        hg_send[i] = dot(w_ref[band, :], og_ref[...], NT).astype(jnp.bfloat16)
        return carry

    for i in range(1, M):
        share(i, 0)
        h_copy(i).start()
    share(0, 0)

    numer[...] = jnp.zeros_like(numer)
    denom[...] = jnp.zeros_like(denom)
    key_pos = lax.broadcasted_iota(jnp.int32, (tokens, tokens), 0)
    query_pos = lax.broadcasted_iota(jnp.int32, (tokens, tokens), 1)
    causal = key_pos <= query_pos
    for g in range(group):
        lanes = slice(g * HD, (g + 1) * HD)
        score = dot(k_ref[...], q_ref[:, lanes], NT)
        exp = jnp.exp(softcap * jnp.tanh(score * (qscale / softcap)))
        exp = jnp.where(causal, exp, 0.0)
        denom[x, g : g + 1, :] = jnp.sum(exp, axis=0, keepdims=True)
        numer[x, lanes, :] = dot(v_ref[...], exp.astype(jnp.bfloat16), TN)

    def pick(code, way, step, kind):
        return choose(
            code == 2, slab[way, step, kind, BLOCK:, :], slab[way, step, kind, :BLOCK, :]
        )

    def forward(step):
        def request(r, carry):
            code_a, code_b = table[0, r, step], table[1, r, step]
            keys = jnp.concatenate(
                [pick(code_a, 0, step, KEY), pick(code_b, 1, step, KEY)], axis=0
            )
            val_a, val_b = pick(code_a, 0, step, VALUE), pick(code_b, 1, step, VALUE)
            zero = jnp.zeros_like(val_a)
            vals = jnp.concatenate(
                [choose(code_a > 0, val_a, zero), choose(code_b > 0, val_b, zero)], axis=0
            )
            for g in range(group):
                lanes = slice(g * HD, (g + 1) * HD)
                tanh = jnp.tanh(dot(keys, queries[r, :, lanes], NT) * (qscale / softcap))
                exp = jnp.exp(softcap * tanh)
                half = exp.astype(jnp.bfloat16)
                exps[step - 1, r, g] = half
                slopes[step - 1, r, g] = (exp * (1.0 - tanh * tanh)).astype(jnp.bfloat16)
                sum_a = jnp.sum(exp[:BLOCK], axis=0, keepdims=True)
                sum_b = jnp.sum(exp[BLOCK:], axis=0, keepdims=True)
                none = jnp.zeros_like(sum_a)
                denom[r, g : g + 1, :] += choose(code_a > 0, sum_a, none) + choose(
                    code_b > 0, sum_b, none
                )
                numer[r, lanes, :] += dot(vals, half, TN)
            return carry

        lax.fori_loop(0, X, request, 0)

    live = lax.broadcasted_iota(jnp.int32, (group * HD, tokens), 1) < token_count[0]

    def gather_step(step, carry):
        for kind in (KEY, VALUE):
            for way in (RIGHT, LEFT):
                last = last_hop(way, kind)

                @pl.when(step <= last)
                def _():
                    gather_hop(way, kind, step).wait_recv()

                @pl.when(step < last)
                def _():
                    gather_hop(way, kind, step + 1).start()

        @pl.when(step == lag + 1)
        def _():
            for i in range(1, X):
                q_copy(i).wait_recv()

        @pl.when(step > lag)
        def _():
            forward(step - lag)

        @pl.when(step == min(lag + 3, H))
        def _():
            total = hg_send[0].astype(jnp.float32)
            for i in range(1, M):
                h_copy(i).wait_recv()
                total += hg_recv[i].astype(jnp.float32)
            heads_grad[x] = jnp.where(live, total, 0.0).astype(jnp.bfloat16)
            for i in range(1, X):
                g_copy(i).start()

        return carry

    lax.fori_loop(1, H + 1, gather_step, 0)

    def late(step, carry):
        forward(step)
        return carry

    lax.fori_loop(H + 1 - lag, H + 1, late, 0)

    for i in range(1, X):
        g_copy(i).wait_recv()
    for r in range(X):
        for g in range(group):
            lanes = slice(g * HD, (g + 1) * HD)
            row = (r * group + g) * 2
            stat_send[row : row + 1, :] = denom[r, g : g + 1, :]
            stat_send[row + 1 : row + 2, :] = jnp.sum(
                heads_grad[r, lanes, :].astype(jnp.float32) * numer[r, lanes, :],
                axis=0,
                keepdims=True,
            )
    for i in range(1, X):
        s_copy(i).start()
    num_send[...] = numer[...].astype(jnp.bfloat16)
    for i in range(1, X):
        n_copy(i).start()
    ring_recv[RIGHT, H - 1, VALUE] = jnp.zeros_like(ring_recv[RIGHT, H - 1, VALUE])
    ring_recv[LEFT, H - 1, KEY] = jnp.zeros_like(ring_recv[LEFT, H - 1, KEY])
    stats = stat_send[...]
    for i in range(1, X):
        s_copy(i).wait_recv()
        stats += stat_recv[i]
    for r in range(X):
        for g in range(group):
            lanes = slice(g * HD, (g + 1) * HD)
            row = (r * group + g) * 2
            inverse = 1.0 / stats[row : row + 1, :]
            rows[r, 2 * g : 2 * g + 1, :] = inverse
            rows[r, 2 * g + 1 : 2 * g + 2, :] = inverse * stats[row + 1 : row + 2, :]
            scaled_grad[r, lanes, :] = (
                heads_grad[r, lanes, :].astype(jnp.float32) * inverse
            ).astype(jnp.bfloat16)

    def backward(dist):
        part[...] = jnp.zeros_like(part)

        def request(r, carry):
            code_a, code_b = table[0, r, dist], table[1, r, dist]
            vals = jnp.concatenate(
                [pick(code_a, 0, dist, VALUE), pick(code_b, 1, dist, VALUE)], axis=0
            )
            key_grad = jnp.zeros((2 * BLOCK, HD), jnp.float32)
            value_grad = jnp.zeros((2 * BLOCK, HD), jnp.float32)
            for g in range(group):
                lanes = slice(g * HD, (g + 1) * HD)
                inverse = rows[r, 2 * g : 2 * g + 1, :]
                delta = rows[r, 2 * g + 1 : 2 * g + 2, :]
                dprob = dot(vals, heads_grad[r, lanes, :], NN)
                slope = slopes[dist - 1, r, g].astype(jnp.float32)
                dscore = slope * ((dprob - delta) * (inverse * qscale))
                key_grad += dot(dscore.astype(jnp.bfloat16), queries[r, :, lanes], NN)
                value_grad += dot(exps[dist - 1, r, g], scaled_grad[r, lanes, :], NT)
            none = jnp.zeros((BLOCK, HD), jnp.float32)
            for side, code in enumerate((code_a, code_b)):
                span = slice(side * BLOCK, (side + 1) * BLOCK)
                for block in range(2):
                    place = slice(block * BLOCK, (block + 1) * BLOCK)
                    hit = code == block + 1
                    part[side, KEY, place, :] += choose(hit, key_grad[span], none)
                    part[side, VALUE, place, :] += choose(hit, value_grad[span], none)
            return carry

        lax.fori_loop(0, X, request, 0)

    def scatter_step(index, carry):
        dist = H - index
        backward(dist)

        @pl.when(index == 0)
        def _():
            own_sum[...] = part[1]
            ring_send[RIGHT, H, KEY] = part[0, KEY].astype(jnp.bfloat16)
            ring_send[LEFT, H, VALUE] = part[0, VALUE].astype(jnp.bfloat16)
            ring_hop(RIGHT, KEY, H).start()
            ring_hop(LEFT, VALUE, H).start()

        @pl.when(index > 0)
        def _():
            for kind in (KEY, VALUE):
                for way in (RIGHT, LEFT):

                    @pl.when(dist + 1 <= last_hop(way, kind))
                    def _():
                        ring_hop(way, kind, dist + 1).wait_recv()

                    ring_send[way, dist, kind] = (
                        part[1 - way, kind] + ring_recv[way, dist, kind].astype(jnp.float32)
                    ).astype(jnp.bfloat16)
                    ring_hop(way, kind, dist).start()

        @pl.when(index == min(3, H - 1))
        def _():
            total = numer[x]
            for i in range(1, X):
                n_copy(i).wait_recv()
                total += num_recv[i].astype(jnp.float32)
            out = jnp.concatenate(
                [total[g * HD : (g + 1) * HD] * rows[x, 2 * g : 2 * g + 1, :] for g in range(group)],
                axis=0,
            )
            heads[m] = jnp.where(live, out, 0.0).T.astype(jnp.bfloat16)
            for i in range(1, M):
                a_copy(i).start()

        return carry

    lax.fori_loop(0, H, scatter_step, 0)

    for i in range(1, M):
        a_copy(i).wait_recv()
    attn_ref[...] = dot(heads[0], w_ref[: group * HD, :], NN)

    def project(j, carry):
        band = pl.ds(pl.multiple_of(j * (group * HD), group * HD), group * HD)
        attn_ref[...] += dot(heads[j], w_ref[band, :], NN)
        return carry

    lax.fori_loop(1, M, project, 0)

    for kind in (KEY, VALUE):
        total = own_sum[kind]
        for way in (RIGHT, LEFT):
            ring_hop(way, kind, 1).wait_recv()
            total += ring_recv[way, 0, kind].astype(jnp.float32)
        grad_ref[kind] = total

    for kind in (KEY, VALUE):
        for way in (RIGHT, LEFT):
            for hop in range(1, last_hop(way, kind) + 1):
                gather_hop(way, kind, hop).wait_send()
                ring_hop(way, kind, hop).wait_send()
    for i in range(1, X):
        q_copy(i).wait_send()
        g_copy(i).wait_send()
        s_copy(i).wait_send()
        n_copy(i).wait_send()
    for i in range(1, M):
        h_copy(i).wait_send()
        a_copy(i).wait_send()


def local(
    Z,
    X,
    queries,
    keys,
    values,
    out_weight,
    out_grad,
    bank,
    moment_one,
    moment_two,
    block_list,
    block_count,
    token_count,
):
    M = lax.axis_size("mp")
    H = Z // 2
    lag = 2 if H > 3 else 1
    req = lax.axis_index("req")
    z, x = req // X, req % X
    tokens, heads_width = queries.shape
    group = heads_width // HD
    width = out_weight.shape[1]
    blk_dev = bank.shape[0] // BLOCK

    lists = lax.dynamic_slice_in_dim(block_list, z * X, X, 0)
    counts = lax.dynamic_slice_in_dim(block_count, z * X, X, 0)
    steps = jnp.arange(H + 1, dtype=jnp.int32)
    behind = ((z - steps) % Z) * X + x
    ahead = jnp.where(steps == H, z, (z + steps) % Z) * X + x
    owners = jnp.stack([behind, ahead])
    used = lax.broadcasted_iota(jnp.int32, lists.shape, 1) < counts[:, None]
    hit = used[None, :, None, :] & (lists[None, :, None, :] // blk_dev == owners[:, None, :, None])
    table = jnp.sum(jnp.where(hit, 1 + lists[None, :, None, :] % blk_dev, 0), axis=-1)

    own = jnp.transpose(bank.astype(jnp.bfloat16), (1, 0, 2))
    bf16, f32 = jnp.bfloat16, jnp.float32
    rows_local = bank.shape[0]
    vmem = pltpu.VMEM
    dma = pltpu.SemaphoreType.DMA
    smem_spec = pl.BlockSpec(memory_space=pltpu.SMEM)
    vmem_spec = pl.BlockSpec(memory_space=pltpu.VMEM)
    attn_out, grad = pl.pallas_call(
        functools.partial(step_kernel, (Z, X, M, lag)),
        out_shape=(
            jax.ShapeDtypeStruct((tokens, width), f32),
            jax.ShapeDtypeStruct((2, rows_local, HD), f32),
        ),
        in_specs=[smem_spec, smem_spec] + [vmem_spec] * 6,
        out_specs=(vmem_spec, vmem_spec),
        scratch_shapes=[
            vmem((2, H + 1, 2, rows_local, HD), bf16),
            vmem((X, tokens, heads_width), bf16),
            vmem((X, heads_width, tokens), bf16),
            vmem((X, heads_width, tokens), bf16),
            vmem((H, X, group, 2 * BLOCK, tokens), bf16),
            vmem((H, X, group, 2 * BLOCK, tokens), bf16),
            vmem((X, heads_width, tokens), f32),
            vmem((X, group, tokens), f32),
            vmem((M, heads_width, tokens), bf16),
            vmem((M, heads_width, tokens), bf16),
            vmem((2 * X * group, tokens), f32),
            vmem((X, 2 * X * group, tokens), f32),
            vmem((X, 2 * group, tokens), f32),
            vmem((X, heads_width, tokens), bf16),
            vmem((X, heads_width, tokens), bf16),
            vmem((M, tokens, heads_width), bf16),
            vmem((2, 2, rows_local, HD), f32),
            vmem((2, rows_local, HD), f32),
            vmem((2, H + 1, 2, rows_local, HD), bf16),
            vmem((2, H + 1, 2, rows_local, HD), bf16),
            dma((2, H + 1, 2)),
            dma((2, H + 1, 2)),
            dma((X,)),
            dma((X,)),
            dma((X,)),
            dma((X,)),
            dma((M,)),
            dma((M,)),
            dma((X,)),
            dma((X,)),
            dma((X,)),
            dma((X,)),
            dma((M,)),
            dma((M,)),
            dma((2, H + 1, 2)),
            dma((2, H + 1, 2)),
        ],
        compiler_params=pltpu.CompilerParams(
            collective_id=0, has_side_effects=True, vmem_limit_bytes=56 << 20
        ),
    )(table, token_count, own, queries, keys, values, out_weight, out_grad)

    block_grad = jnp.transpose(grad, (1, 0, 2))
    moment_next = beta_one * moment_one + (1.0 - beta_one) * block_grad
    second_next = beta_two * moment_two + (1.0 - beta_two) * block_grad * block_grad
    bank_next = bank - learn_rate * (moment_next / bias_one) / (
        jnp.sqrt(second_next / bias_two) + adam_eps
    )
    return (attn_out, bank_next, moment_next, second_next)


def solution(mesh):
    reqs = mesh.shape["req"]
    X = 4 if reqs >= 64 else 2
    return jax.shard_map(
        functools.partial(local, reqs // X, X),
        mesh=mesh,
        in_specs=(
            P("req", "mp"),
            P("req", "mp"),
            P("req", "mp"),
            P(None, "mp"),
            P("req", "mp"),
            P("req", None, "mp"),
            P("req", None, "mp"),
            P("req", None, "mp"),
            P(),
            P(),
            P("req"),
        ),
        out_specs=(
            P("req", "mp"),
            P("req", None, "mp"),
            P("req", None, "mp"),
            P("req", None, "mp"),
        ),
        check_vma=False,
    )
```

time: 774 us -> 115 us (0.15)
  waiting for transfers between devices: 550 us -> 0 us
  Pallas kernels: 0 us -> 96 us
  matrix products: 83.6 us -> 0 us
  local copies, waits for them, and re-layouts: 58.7 us -> 14.2 us
  other arithmetic: 38 us -> 1.7 us
  starting transfers between devices: 25.3 us -> 0 us
  between operations: 15 us -> 1.35 us
    all_to_all x2 -> x0, waiting for transfers between devices: 517 us -> none  [the longest x1 332 us: local(): lax.all_to_all(to_slots(stacked, holder, owners), 'req', split_axis=0, co...]
    pallas_call x0 -> x1, Pallas kernels: none -> 96 us  [local(): pl.pallas_call(functools.partial(step_kernel, (Z, X, M, lag)), out_shape=...]
    dot_general x46 -> x0, matrix products: 83.6 us -> none  [the longest x17 21 us: key_scores(): jnp.einsum('tkgd,skd->kgts', query_four, key_three, preferred_element_typ...]
    reshape x8 -> x0, local copies, waits for them, and re-layouts: 43.1 us -> none  [the longest x2 13 us: local(): outgoing = outgoing.reshape(owners, BLOCK, 2, keys.shape[1])]
    all_gather x1 -> x0, waiting for transfers between devices: 33.6 us -> none  [local(): lax.all_gather(heads_out, 'mp', axis=1, tiled=True)]
    all_to_all x2 -> x0, starting transfers between devices: 25.2 us -> none  [the longest x1 19 us: local(): lax.all_to_all(outgoing, 'req', split_axis=0, concat_axis=0, tiled=True)]
    lt x25 -> x1, other arithmetic: 20 us -> 0.08 us  [local(): used = lax.broadcasted_iota(jnp.int32, lists.shape, 1) < counts[:, None]]
    unnamed x25 -> x16, local copies, waits for them, and re-layouts: 0.61 us -> 12.7 us
  transfers between devices with their start and end apart: 4 -> 0, of which waited for: 3 -> 0; matrix products, arithmetic and copies ran while one was open for 6% -> 0% of each run, Pallas kernels for 0% -> 0%
where the time goes in v1:
time: 115 us; the launch traced here: 113 us
  Pallas kernels  96 us (83%)
  local copies, waits for them, and re-layouts  14.2 us (12%)
  other arithmetic  1.7 us (1%)
  between operations  1.35 us (1%)
    pallas_call x1, Pallas kernels, local(): pl.pallas_call(functools.partial(step_kernel, (Z, X, M, lag)), out_shape=...  96 us
    unnamed x16, local copies, waits for them, and re-layouts  12.7 us

profile of v1, /device:TPU:24, one launch (start us, length us, event | category | flops | bytes accessed | tf_op | source)
XLA Modules:
  0.0 113.3 jit_solution(5183283006641291789)
XLA Ops:
  0.6 0.0 copy-start
  1.4 0.7 dynamic_slice.6
  2.1 0.1 iota_compare_fusion
  2.2 0.0 copy-done
  2.2 0.1 constant_dynamic-slice_fusion
  2.2 0.1 copy.52
  2.3 0.4 select_reduce_fusion
  2.8 0.7 copy.42.table
  3.5 1.6 %copy.65 = bf16[256,2,128]{2,0,1:T(8,128)(2,1)} copy(f32[256,2,128]{2,1,0:T(2,128)} %param.16) | data formatting | bytes 393216 | tf_op args[5]
  5.1 1.9 %copy.44.og_ref = bf16[256,576]{1,0:T(8,128)(2,1)} copy(bf16[256,576]{0,1:T(8,128)(2,1)} %param.15) | data formatting | bytes 589824 | tf_op args[4]
  7.0 4.3 %copy.43.w_ref = bf16[2048,576]{1,0:T(8,128)(2,1)} copy(bf16[2048,576]{0,1:T(8,128)(2,1)} %param.14) | data formatting | bytes 4718592 | tf_op args[3]
  11.3 0.0 copy-start.1
  11.3 0.0 copy-start.2
  11.3 0.0 copy-start.3
  11.3 96.0 %shard_map.138 = (f32[256,576]{1,0:T(8,128)}, f32[2,256,128]{2,1,0:T(8,128)}) custom-call(s32[2,4,9]{2,1,0:T(4,128)} %copy.42.table, s32[1]{0:T(128)S(6)} %copy.66.token_count, bf16[2,256,128]{2,1,0:T(8,128)(2,1)} %bitcast.10, bf16[256,256]{1,0:T(8,128)(2,1)} %q_ref.1, bf16[256,128]{1,0:T(8,128)(2,1)} %k_ref.1, bf16[256,128]{1,0:T(8,128)(2,1)} %v_ref.1, ...), custom_call_target="tpu_custom_call" | custom-call | tf_op jit(solution)/shard_map/pallas_call | solution.py:467
  107.3 2.1 %copy.48 = f32[256,576]{0,1:T(8,128)} copy(f32[256,576]{1,0:T(8,128)} %get-tuple-element.16) | data formatting | bytes 1179648
  109.5 0.0 copy-done.1
  109.5 0.0 copy-done.2
  109.5 0.0 copy-done.3
  109.5 1.1 %divide_subtract_fusion = (f32[256,2,128]{2,0,1:T(8,128)S(1)}, f32[256,2,128]{2,0,1:T(8,128)S(1)}, f32[256,2,128]{2,0,1:T(8,128)S(1)}) fusion(f32[256,2,128]{2,1,0:T(2,128)S(1)} %copy-done.1, f32[2,256,128]{2,1,0:T(8,128)} %get-tuple-element.7, f32[256,2,128]{2,1,0:T(2,128)S(1)} %copy-done.2, f32[256,2,128]{2,1,0:T(2,128)S(1)} %copy-done.3), kind=kLoop, calls=%fused_computation.6 | loop fusion | flops 786432 | bytes 1835008 | tf_op jit(solution)/shard_map/sub | solution.py:521
  110.6 0.9 copy.49
  111.5 0.9 copy.50
  112.4 0.9 copy.51
  (3 shorter events, 0.0 us)
Async XLA Ops:
  0.6 1.5 %copy-start = (s32[64,32]{0,1:T(8,128)S(1)}, s32[64,32]{0,1:T(8,128)}, u32[]{:S(2)}) copy-start(s32[64,32]{0,1:T(8,128)} %param.19) | copy-start | bytes 24580
  11.3 98.2 %copy-start.1 = (f32[256,2,128]{2,1,0:T(2,128)S(1)}, f32[256,2,128]{2,1,0:T(2,128)}, u32[]{:S(2)}) copy-start(f32[256,2,128]{2,1,0:T(2,128)} %param.16) | copy-start | bytes 786436
  11.3 98.2 %copy-start.2 = (f32[256,2,128]{2,1,0:T(2,128)S(1)}, f32[256,2,128]{2,1,0:T(2,128)}, u32[]{:S(2)}) copy-start(f32[256,2,128]{2,1,0:T(2,128)} %param.17) | copy-start | bytes 786436
  11.3 98.2 %copy-start.3 = (f32[256,2,128]{2,1,0:T(2,128)S(1)}, f32[256,2,128]{2,1,0:T(2,128)}, u32[]{:S(2)}) copy-start(f32[256,2,128]{2,1,0:T(2,128)} %param.18) | copy-start | bytes 786436

commit v2 on v1

--- a/solution.py
+++ b/solution.py
@@ -38,7 +38,7 @@
     sizes,
     table,
     token_count,
-    own_ref,
+    bank_ref,
     q_ref,
     k_ref,
     v_ref,
@@ -83,7 +83,7 @@
     rs_send_sem,
     rs_recv_sem,
 ):
-    Z, X, M, lag = sizes
+    Z, X, M = sizes
     H = Z // 2
     tokens = q_ref.shape[0]
     group = q_ref.shape[1] // HD
@@ -109,15 +109,16 @@
             device_id_type=pl.DeviceIdType.MESH,
         )
 
-    def gather_hop(way, kind, hop):
+    def gather_hop(way, kind, half, hop):
         lane = way
         if way == LEFT and kind == VALUE:
             lane = 1 - hop // H
+        span = pl.ds(half * BLOCK, BLOCK)
         return remote(
-            slab.at[way, hop - 1, kind],
-            slab.at[lane, hop, kind],
-            ag_send_sem.at[way, hop, kind],
-            ag_recv_sem.at[way, hop, kind],
+            slab.at[way, hop - 1, kind, span],
+            slab.at[lane, hop, kind, span],
+            ag_send_sem.at[way, hop, 2 * kind + half],
+            ag_recv_sem.at[way, hop, 2 * kind + half],
             toward[way],
         )
 
@@ -150,12 +151,13 @@
     def a_copy(i):
         return remote(heads.at[m], heads.at[m], a_send_sem.at[i], a_recv_sem.at[i], m_peer(i))
 
-    def ring_hop(way, kind, dist):
+    def ring_hop(way, kind, half, dist):
+        span = pl.ds(half * BLOCK, BLOCK)
         return remote(
-            ring_send.at[way, dist, kind],
-            ring_recv.at[way, dist - 1, kind],
-            rs_send_sem.at[way, dist, kind],
-            rs_recv_sem.at[way, dist, kind],
+            ring_send.at[way, dist, kind, span],
+            ring_recv.at[way, dist - 1, kind, span],
+            rs_send_sem.at[way, dist, 2 * kind + half],
+            rs_recv_sem.at[way, dist, 2 * kind + half],
             toward[way],
         )
 
@@ -165,29 +167,35 @@
         pl.semaphore_signal(
             barrier, inc=1, device_id=partner, device_id_type=pl.DeviceIdType.MESH
         )
-    own = own_ref[...]
-    slab[RIGHT, 0] = own
-    slab[LEFT, 0] = own
-    slab[LEFT, H] = own
+    for kind in (KEY, VALUE):
+        own = bank_ref[pl.ds(kind, 2 * BLOCK, stride=2), :].astype(jnp.bfloat16)
+        slab[RIGHT, 0, kind] = own
+        slab[LEFT, 0, kind] = own
+        slab[LEFT, H, kind] = own
     queries[x] = q_ref[...]
     pl.semaphore_wait(barrier, len(partners))
 
+    near = [i for i in range(1, X) if i in (1, X - 1)]
+    far = [i for i in range(1, X) if i not in near]
+    order = [0] + near + far
     for kind in (KEY, VALUE):
-        for way in (RIGHT, LEFT):
-            gather_hop(way, kind, 1).start()
-    for i in range(1, X):
+        for half in range(2):
+            for way in (RIGHT, LEFT):
+                gather_hop(way, kind, half, 1).start()
+    for i in order[1:]:
         q_copy(i).start()
 
-    def share(i, carry):
+    og = og_ref[...].T
+
+    def share(i):
         target = (m + i) % M
         band = pl.ds(pl.multiple_of(target * (group * HD), group * HD), group * HD)
-        hg_send[i] = dot(w_ref[band, :], og_ref[...], NT).astype(jnp.bfloat16)
-        return carry
+        hg_send[i] = dot(og, w_ref[:, band], NN).astype(jnp.bfloat16)
 
     for i in range(1, M):
-        share(i, 0)
+        share(i)
         h_copy(i).start()
-    share(0, 0)
+    share(0)
 
     numer[...] = jnp.zeros_like(numer)
     denom[...] = jnp.zeros_like(denom)
@@ -207,8 +215,9 @@
             code == 2, slab[way, step, kind, BLOCK:, :], slab[way, step, kind, :BLOCK, :]
         )
 
-    def forward(step):
-        def request(r, carry):
+    def forward(step, offsets):
+        for offset in offsets:
+            r = (x + offset) % X
             code_a, code_b = table[0, r, step], table[1, r, step]
             keys = jnp.concatenate(
                 [pick(code_a, 0, step, KEY), pick(code_b, 1, step, KEY)], axis=0
@@ -218,11 +227,13 @@
             vals = jnp.concatenate(
                 [choose(code_a > 0, val_a, zero), choose(code_b > 0, val_b, zero)], axis=0
             )
+            halves = []
             for g in range(group):
                 lanes = slice(g * HD, (g + 1) * HD)
                 tanh = jnp.tanh(dot(keys, queries[r, :, lanes], NT) * (qscale / softcap))
                 exp = jnp.exp(softcap * tanh)
                 half = exp.astype(jnp.bfloat16)
+                halves.append(half)
                 exps[step - 1, r, g] = half
                 slopes[step - 1, r, g] = (exp * (1.0 - tanh * tanh)).astype(jnp.bfloat16)
                 sum_a = jnp.sum(exp[:BLOCK], axis=0, keepdims=True)
@@ -231,54 +242,66 @@
                 denom[r, g : g + 1, :] += choose(code_a > 0, sum_a, none) + choose(
                     code_b > 0, sum_b, none
                 )
-                numer[r, lanes, :] += dot(vals, half, TN)
-            return carry
-
-        lax.fori_loop(0, X, request, 0)
+            mixed = dot(vals, jnp.concatenate(halves, axis=1), TN)
+            for g in range(group):
+                numer[r, g * HD : (g + 1) * HD, :] += mixed[:, g * tokens : (g + 1) * tokens]
 
     live = lax.broadcasted_iota(jnp.int32, (group * HD, tokens), 1) < token_count[0]
-
-    def gather_step(step, carry):
-        for kind in (KEY, VALUE):
+    early, late = order[: X // 2], order[X // 2 :]
+
+    def pass_on(step, kind):
+        for half in range(2):
             for way in (RIGHT, LEFT):
                 last = last_hop(way, kind)
 
                 @pl.when(step <= last)
                 def _():
-                    gather_hop(way, kind, step).wait_recv()
+                    gather_hop(way, kind, half, step).wait_recv()
 
                 @pl.when(step < last)
                 def _():
-                    gather_hop(way, kind, step + 1).start()
-
-        @pl.when(step == lag + 1)
-        def _():
-            for i in range(1, X):
-                q_copy(i).wait_recv()
-
-        @pl.when(step > lag)
-        def _():
-            forward(step - lag)
-
-        @pl.when(step == min(lag + 3, H))
+                    gather_hop(way, kind, half, step + 1).start()
+
+    def gather_step(step, carry):
+        @pl.when(step <= H)
+        def _():
+            pass_on(step, KEY)
+
+        @pl.when(step == 2)
+        def _():
+            for i in late:
+                q_copy(X - i).wait_recv()
+
+        @pl.when(step > 1)
+        def _():
+            forward(step - 1, late)
+
+        @pl.when(step <= H)
+        def _():
+            pass_on(step, VALUE)
+
+        @pl.when(step == 1)
+        def _():
+            for i in early[1:]:
+                q_copy(X - i).wait_recv()
+
+        @pl.when(step <= H)
+        def _():
+            forward(step, early)
+
+        @pl.when(step == min(6, H))
         def _():
             total = hg_send[0].astype(jnp.float32)
             for i in range(1, M):
                 h_copy(i).wait_recv()
                 total += hg_recv[i].astype(jnp.float32)
-            heads_grad[x] = jnp.where(live, total, 0.0).astype(jnp.bfloat16)
-            for i in range(1, X):
+            heads_grad[x] = jnp.where(live, total.T, 0.0).astype(jnp.bfloat16)
+            for i in order[1:]:
                 g_copy(i).start()
 
         return carry
 
-    lax.fori_loop(1, H + 1, gather_step, 0)
-
-    def late(step, carry):
-        forward(step)
-        return carry
-
-    lax.fori_loop(H + 1 - lag, H + 1, late, 0)
+    lax.fori_loop(1, H + 2, gather_step, 0)
 
     for i in range(1, X):
         g_copy(i).wait_recv()
@@ -292,10 +315,10 @@
                 axis=0,
                 keepdims=True,
             )
-    for i in range(1, X):
+    for i in order[1:]:
         s_copy(i).start()
     num_send[...] = numer[...].astype(jnp.bfloat16)
-    for i in range(1, X):
+    for i in order[1:]:
         n_copy(i).start()
     ring_recv[RIGHT, H - 1, VALUE] = jnp.zeros_like(ring_recv[RIGHT, H - 1, VALUE])
     ring_recv[LEFT, H - 1, KEY] = jnp.zeros_like(ring_recv[LEFT, H - 1, KEY])
@@ -314,10 +337,10 @@
                 heads_grad[r, lanes, :].astype(jnp.float32) * inverse
             ).astype(jnp.bfloat16)
 
-    def backward(dist):
-        part[...] = jnp.zeros_like(part)
-
-        def request(r, carry):
+    def backward(dist, requests, first):
+        slot = dist % 2
+        found = []
+        for r in requests:
             code_a, code_b = table[0, r, dist], table[1, r, dist]
             vals = jnp.concatenate(
                 [pick(code_a, 0, dist, VALUE), pick(code_b, 1, dist, VALUE)], axis=0
@@ -333,45 +356,70 @@
                 dscore = slope * ((dprob - delta) * (inverse * qscale))
                 key_grad += dot(dscore.astype(jnp.bfloat16), queries[r, :, lanes], NN)
                 value_grad += dot(exps[dist - 1, r, g], scaled_grad[r, lanes, :], NT)
-            none = jnp.zeros((BLOCK, HD), jnp.float32)
-            for side, code in enumerate((code_a, code_b)):
-                span = slice(side * BLOCK, (side + 1) * BLOCK)
+            found.append(((code_a, code_b), (key_grad, value_grad)))
+        none = jnp.zeros((BLOCK, HD), jnp.float32)
+        for side in range(2):
+            span = slice(side * BLOCK, (side + 1) * BLOCK)
+            for kind in (KEY, VALUE):
                 for block in range(2):
                     place = slice(block * BLOCK, (block + 1) * BLOCK)
-                    hit = code == block + 1
-                    part[side, KEY, place, :] += choose(hit, key_grad[span], none)
-                    part[side, VALUE, place, :] += choose(hit, value_grad[span], none)
-            return carry
-
-        lax.fori_loop(0, X, request, 0)
+                    total = none if first else part[slot, side, kind, place, :]
+                    for codes, grads in found:
+                        total += choose(codes[side] == block + 1, grads[kind][span], none)
+                    part[slot, side, kind, place, :] = total
+
+    def hand_over(dist, kind):
+        slot = dist % 2
+        for half in range(2):
+            span = slice(half * BLOCK, (half + 1) * BLOCK)
+            for way in (RIGHT, LEFT):
+                last = last_hop(way, kind)
+                side = 1 - way
+
+                @pl.when(dist == H)
+                def _():
+                    if way == kind:
+                        ring_send[way, H, kind, span, :] = part[slot, 0, kind, span, :].astype(
+                            jnp.bfloat16
+                        )
+                        ring_hop(way, kind, half, H).start()
+
+                @pl.when(dist < H)
+                def _():
+                    @pl.when(dist < last)
+                    def _():
+                        ring_hop(way, kind, half, dist + 1).wait_recv()
+
+                    ring_send[way, dist, kind, span, :] = (
+                        part[slot, side, kind, span, :]
+                        + ring_recv[way, dist, kind, span, :].astype(jnp.float32)
+                    ).astype(jnp.bfloat16)
+                    ring_hop(way, kind, half, dist).start()
 
     def scatter_step(index, carry):
-        dist = H - index
-        backward(dist)
+        dist = H + 1 - index
+
+        @pl.when(dist <= H)
+        def _():
+            hand_over(dist, KEY)
+
+        @pl.when(dist > 1)
+        def _():
+            backward(dist - 1, range(X // 2), True)
+
+        @pl.when(dist <= H)
+        def _():
+            hand_over(dist, VALUE)
+
+        @pl.when(dist > 1)
+        def _():
+            backward(dist - 1, range(X // 2, X), False)
 
         @pl.when(index == 0)
         def _():
-            own_sum[...] = part[1]
-            ring_send[RIGHT, H, KEY] = part[0, KEY].astype(jnp.bfloat16)
-            ring_send[LEFT, H, VALUE] = part[0, VALUE].astype(jnp.bfloat16)
-            ring_hop(RIGHT, KEY, H).start()
-            ring_hop(LEFT, VALUE, H).start()
-
-        @pl.when(index > 0)
-        def _():
-            for kind in (KEY, VALUE):
-                for way in (RIGHT, LEFT):
-
-                    @pl.when(dist + 1 <= last_hop(way, kind))
-                    def _():
-                        ring_hop(way, kind, dist + 1).wait_recv()
-
-                    ring_send[way, dist, kind] = (
-                        part[1 - way, kind] + ring_recv[way, dist, kind].astype(jnp.float32)
-                    ).astype(jnp.bfloat16)
-                    ring_hop(way, kind, dist).start()
-
-        @pl.when(index == min(3, H - 1))
+            own_sum[...] = part[H % 2, 1]
+
+        @pl.when(index == min(4, H))
         def _():
             total = numer[x]
             for i in range(1, X):
@@ -381,37 +429,37 @@
                 [total[g * HD : (g + 1) * HD] * rows[x, 2 * g : 2 * g + 1, :] for g in range(group)],
                 axis=0,
             )
-            heads[m] = jnp.where(live, out, 0.0).T.astype(jnp.bfloat16)
+            heads[m] = jnp.where(live, out, 0.0).astype(jnp.bfloat16)
             for i in range(1, M):
                 a_copy(i).start()
 
         return carry
 
-    lax.fori_loop(0, H, scatter_step, 0)
+    lax.fori_loop(0, H + 1, scatter_step, 0)
 
     for i in range(1, M):
         a_copy(i).wait_recv()
-    attn_ref[...] = dot(heads[0], w_ref[: group * HD, :], NN)
-
-    def project(j, carry):
-        band = pl.ds(pl.multiple_of(j * (group * HD), group * HD), group * HD)
-        attn_ref[...] += dot(heads[j], w_ref[band, :], NN)
-        return carry
-
-    lax.fori_loop(1, M, project, 0)
+    depth = group * HD
+    total = dot(w_ref[:, :depth], heads[0], NN)
+    for j in range(1, M):
+        total += dot(w_ref[:, j * depth : (j + 1) * depth], heads[j], NN)
+    attn_ref[...] = total
 
     for kind in (KEY, VALUE):
+        for half in range(2):
+            for way in (RIGHT, LEFT):
+                ring_hop(way, kind, half, 1).wait_recv()
         total = own_sum[kind]
         for way in (RIGHT, LEFT):
-            ring_hop(way, kind, 1).wait_recv()
             total += ring_recv[way, 0, kind].astype(jnp.float32)
-        grad_ref[kind] = total
+        grad_ref[pl.ds(kind, 2 * BLOCK, stride=2), :] = total
 
     for kind in (KEY, VALUE):
         for way in (RIGHT, LEFT):
             for hop in range(1, last_hop(way, kind) + 1):
-                gather_hop(way, kind, hop).wait_send()
-                ring_hop(way, kind, hop).wait_send()
+                for half in range(2):
+                    gather_hop(way, kind, half, hop).wait_send()
+                    ring_hop(way, kind, half, hop).wait_send()
     for i in range(1, X):
         q_copy(i).wait_send()
         g_copy(i).wait_send()
@@ -439,7 +487,6 @@
 ):
     M = lax.axis_size("mp")
     H = Z // 2
-    lag = 2 if H > 3 else 1
     req = lax.axis_index("req")
     z, x = req // X, req % X
     tokens, heads_width = queries.shape
@@ -457,7 +504,7 @@
     hit = used[None, :, None, :] & (lists[None, :, None, :] // blk_dev == owners[:, None, :, None])
     table = jnp.sum(jnp.where(hit, 1 + lists[None, :, None, :] % blk_dev, 0), axis=-1)
 
-    own = jnp.transpose(bank.astype(jnp.bfloat16), (1, 0, 2))
+    flat = (2 * bank.shape[0], HD)
     bf16, f32 = jnp.bfloat16, jnp.float32
     rows_local = bank.shape[0]
     vmem = pltpu.VMEM
@@ -465,10 +512,10 @@
     smem_spec = pl.BlockSpec(memory_space=pltpu.SMEM)
     vmem_spec = pl.BlockSpec(memory_space=pltpu.VMEM)
     attn_out, grad = pl.pallas_call(
-        functools.partial(step_kernel, (Z, X, M, lag)),
+        functools.partial(step_kernel, (Z, X, M)),
         out_shape=(
-            jax.ShapeDtypeStruct((tokens, width), f32),
-            jax.ShapeDtypeStruct((2, rows_local, HD), f32),
+            jax.ShapeDtypeStruct((width, tokens), f32),
+            jax.ShapeDtypeStruct(flat, f32),
         ),
         in_specs=[smem_spec, smem_spec] + [vmem_spec] * 6,
         out_specs=(vmem_spec, vmem_spec),
@@ -481,20 +528,20 @@
             vmem((H, X, group, 2 * BLOCK, tokens), bf16),
             vmem((X, heads_width, tokens), f32),
             vmem((X, group, tokens), f32),
-            vmem((M, heads_width, tokens), bf16),
-            vmem((M, heads_width, tokens), bf16),
+            vmem((M, tokens, heads_width), bf16),
+            vmem((M, tokens, heads_width), bf16),
             vmem((2 * X * group, tokens), f32),
             vmem((X, 2 * X * group, tokens), f32),
             vmem((X, 2 * group, tokens), f32),
             vmem((X, heads_width, tokens), bf16),
             vmem((X, heads_width, tokens), bf16),
-            vmem((M, tokens, heads_width), bf16),
-            vmem((2, 2, rows_local, HD), f32),
+            vmem((M, heads_width, tokens), bf16),
+            vmem((2, 2, 2, rows_local, HD), f32),
             vmem((2, rows_local, HD), f32),
             vmem((2, H + 1, 2, rows_local, HD), bf16),
             vmem((2, H + 1, 2, rows_local, HD), bf16),
-            dma((2, H + 1, 2)),
-            dma((2, H + 1, 2)),
+            dma((2, H + 1, 4)),
+            dma((2, H + 1, 4)),
             dma((X,)),
             dma((X,)),
             dma((X,)),
@@ -507,21 +554,35 @@
             dma((X,)),
             dma((M,)),
             dma((M,)),
-            dma((2, H + 1, 2)),
-            dma((2, H + 1, 2)),
+            dma((2, H + 1, 4)),
+            dma((2, H + 1, 4)),
         ],
         compiler_params=pltpu.CompilerParams(
             collective_id=0, has_side_effects=True, vmem_limit_bytes=56 << 20
         ),
-    )(table, token_count, own, queries, keys, values, out_weight, out_grad)
-
-    block_grad = jnp.transpose(grad, (1, 0, 2))
-    moment_next = beta_one * moment_one + (1.0 - beta_one) * block_grad
-    second_next = beta_two * moment_two + (1.0 - beta_two) * block_grad * block_grad
-    bank_next = bank - learn_rate * (moment_next / bias_one) / (
+    )(
+        table,
+        token_count,
+        bank.reshape(flat),
+        queries,
+        keys,
+        values,
+        out_weight.T,
+        out_grad.T,
+    )
+
+    one, two = moment_one.reshape(flat), moment_two.reshape(flat)
+    moment_next = beta_one * one + (1.0 - beta_one) * grad
+    second_next = beta_two * two + (1.0 - beta_two) * grad * grad
+    bank_next = bank.reshape(flat) - learn_rate * (moment_next / bias_one) / (
         jnp.sqrt(second_next / bias_two) + adam_eps
     )
-    return (attn_out, bank_next, moment_next, second_next)
+    return (
+        attn_out.T,
+        bank_next.reshape(bank.shape),
+        moment_next.reshape(bank.shape),
+        second_next.reshape(bank.shape),
+    )
 
 
 def solution(mesh):

time: 115 us -> 96.1 us (0.84)
  Pallas kernels: 96 us -> 85 us
  local copies, waits for them, and re-layouts: 14.2 us -> 3.51 us
  other arithmetic: 1.7 us -> 4.64 us
    pallas_call x1, Pallas kernels: 96 us -> 85 us  [local(): pl.pallas_call(functools.partial(step_kernel, (Z, X, M)), out_shape=(jax....]
    unnamed x16 -> x6, local copies, waits for them, and re-layouts: 12.7 us -> 2.01 us
    mul x0 -> x2, other arithmetic: none -> 2.17 us  [the longest x1 1.09 us: local(): second_next = beta_two * two + (1.0 - beta_two) * grad * grad]
where the time goes in v2:
time: 96.1 us; the launch traced here: 94.5 us
  Pallas kernels  85 us (88%)
  other arithmetic  4.64 us (5%)
  local copies, waits for them, and re-layouts  3.51 us (4%)
  between operations  1.4 us (1%)
    pallas_call x1, Pallas kernels, local(): pl.pallas_call(functools.partial(step_kernel, (Z, X, M)), out_shape=(jax....  85 us
    unnamed x6, local copies, waits for them, and re-layouts  2.01 us

profile of v2, /device:TPU:24, one launch (start us, length us, event | category | flops | bytes accessed | tf_op | source)
XLA Modules:
  0.0 94.5 jit_solution(18210748908415182881)
XLA Ops:
  0.6 0.0 copy-start
  0.6 0.0 copy-start.1
  1.4 0.7 dynamic_slice.6
  2.1 0.1 iota_compare_fusion
  2.2 0.0 copy-done
  2.2 0.1 constant_dynamic-slice_fusion
  2.3 0.1 copy.22
  2.4 0.4 select_reduce_fusion
  2.8 0.7 copy.21.table
  3.5 1.1 %broadcast_multiply_fusion.1 = f32[256,2,128]{2,1,0:T(2,128)S(1)} fusion(f32[256,2,128]{2,1,0:T(2,128)} %param.17), kind=kLoop, calls=%fused_computation.5 | loop fusion | flops 65536 | bytes 524288 | tf_op jit(solution)/shard_map/mul | solution.py:575
  4.6 1.1 %broadcast_multiply_fusion = f32[256,2,128]{2,1,0:T(2,128)S(1)} fusion(f32[256,2,128]{2,1,0:T(2,128)} %param.18), kind=kLoop, calls=%fused_computation.4 | loop fusion | flops 65536 | bytes 524288 | tf_op jit(solution)/shard_map/mul | solution.py:576
  5.7 85.0 %shard_map.138 = (f32[576,256]{1,0:T(8,128)}, f32[512,128]{1,0:T(8,128)}) custom-call(s32[2,4,9]{2,1,0:T(4,128)} %copy.21.table, s32[1]{0:T(128)S(6)} %copy.24.token_count, f32[512,128]{1,0:T(8,128)} %bitcast.12, bf16[256,256]{1,0:T(8,128)(2,1)} %q_ref.1, bf16[256,128]{1,0:T(8,128)(2,1)} %k_ref.1, bf16[256,128]{1,0:T(8,128)(2,1)} %v_ref.1, ...), custom_call_target="tpu_custom_call" | custom-call | tf_op jit(solution)/shard_map/pallas_call | solution.py:514
  90.7 0.0 copy-done.1
  90.7 1.9 %divide_subtract_fusion = (f32[512,128]{1,0:T(8,128)}, f32[512,128]{1,0:T(8,128)}, f32[512,128]{1,0:T(8,128)}) fusion(f32[512,128]{1,0:T(8,128)S(1)} %bitcast.13, f32[512,128]{1,0:T(8,128)S(1)} %bitcast.10, f32[512,128]{1,0:T(8,128)} %get-tuple-element.7, f32[512,128]{1,0:T(8,128)S(1)} %bitcast.11), kind=kLoop, calls=%fused_computation.2 | loop fusion | flops 655360 | bytes 1835008 | tf_op jit(solution)/shard_map/sub | solution.py:577
  92.6 1.9 %copy.25 = f32[256,576]{0,1:T(8,128)} copy(f32[256,576]{0,1:T(8,128)} %bitcast.14) | data formatting | bytes 1179648
  (3 shorter events, 0.0 us)
Async XLA Ops:
  0.6 1.6 %copy-start = (s32[64,32]{0,1:T(8,128)S(1)}, s32[64,32]{0,1:T(8,128)}, u32[]{:S(2)}) copy-start(s32[64,32]{0,1:T(8,128)} %param.19) | copy-start | bytes 24580
  0.6 90.1 %copy-start.1 = (f32[256,2,128]{2,1,0:T(2,128)S(1)}, f32[256,2,128]{2,1,0:T(2,128)}, u32[]{:S(2)}) copy-start(f32[256,2,128]{2,1,0:T(2,128)} %param.16) | copy-start | bytes 786436

commit v3 on v2

--- a/solution.py
+++ b/solution.py
@@ -11,6 +11,7 @@
 BLOCK = 128
 KEY, VALUE = 0, 1
 RIGHT, LEFT = 0, 1
+AHEAD = 64
 
 softcap = 50.0
 qscale = 1.0 / 12.0
@@ -36,16 +37,22 @@
 
 def step_kernel(
     sizes,
-    table,
+    block_count,
     token_count,
+    lists_ref,
     bank_ref,
     q_ref,
     k_ref,
     v_ref,
+    w_hbm,
+    og_hbm,
+    attn_hbm,
+    grad_ref,
     w_ref,
     og_ref,
     attn_ref,
-    grad_ref,
+    codes,
+    table,
     slab,
     queries,
     heads_grad,
@@ -80,8 +87,8 @@
     n_recv_sem,
     a_send_sem,
     a_recv_sem,
-    rs_send_sem,
     rs_recv_sem,
+    local_sem,
 ):
     Z, X, M = sizes
     H = Z // 2
@@ -156,11 +163,17 @@
         return remote(
             ring_send.at[way, dist, kind, span],
             ring_recv.at[way, dist - 1, kind, span],
-            rs_send_sem.at[way, dist, 2 * kind + half],
+            ag_send_sem.at[way, dist, 2 * kind + half],
             rs_recv_sem.at[way, dist, 2 * kind + half],
             toward[way],
         )
 
+    w_copy = pltpu.make_async_copy(w_hbm, w_ref, local_sem.at[0])
+    og_copy = pltpu.make_async_copy(og_hbm, og_ref, local_sem.at[1])
+    table_copy = pltpu.make_async_copy(codes, table, local_sem.at[2])
+    attn_copy = pltpu.make_async_copy(attn_ref, attn_hbm, local_sem.at[3])
+    og_copy.start()
+    w_copy.start()
     barrier = pltpu.get_barrier_semaphore()
     partners = [right, left] + [x_peer(i) for i in range(1, X)] + [m_peer(i) for i in range(1, M)]
     for partner in partners:
@@ -185,7 +198,9 @@
     for i in order[1:]:
         q_copy(i).start()
 
+    og_copy.wait()
     og = og_ref[...].T
+    w_copy.wait()
 
     def share(i):
         target = (m + i) % M
@@ -210,6 +225,27 @@
         denom[x, g : g + 1, :] = jnp.sum(exp, axis=0, keepdims=True)
         numer[x, lanes, :] = dot(v_ref[...], exp.astype(jnp.bfloat16), TN)
 
+    lists = lists_ref[...]
+    request_lane = lax.broadcasted_iota(jnp.int32, lists.shape, 1)
+    wide = (lists.shape[0], HD)
+    entry = lax.broadcasted_iota(jnp.int32, wide, 0)
+    lane = lax.broadcasted_iota(jnp.int32, wide, 1)
+    is_ahead = lane >= AHEAD
+    place = jnp.where(is_ahead, lane - AHEAD, lane)
+    spot = jnp.where(is_ahead, jnp.where(place == H, z, z + place), z - place + Z)
+    spot = jnp.where(spot >= Z, spot - Z, spot)
+    owner = spot * X + x
+    for r in range(X):
+        column = jnp.sum(
+            jnp.where(request_lane == z * X + r, lists, 0), axis=1, keepdims=True
+        )
+        hit = (entry < block_count[z * X + r]) & (lax.shift_right_logical(column, 1) == owner)
+        codes[r : r + 1, :] = jnp.sum(
+            jnp.where(hit, 1 + (column & 1), 0), axis=0, keepdims=True
+        )
+    table_copy.start()
+    table_copy.wait()
+
     def pick(code, way, step, kind):
         return choose(
             code == 2, slab[way, step, kind, BLOCK:, :], slab[way, step, kind, :BLOCK, :]
@@ -218,7 +254,7 @@
     def forward(step, offsets):
         for offset in offsets:
             r = (x + offset) % X
-            code_a, code_b = table[0, r, step], table[1, r, step]
+            code_a, code_b = table[r, step], table[r, AHEAD + step]
             keys = jnp.concatenate(
                 [pick(code_a, 0, step, KEY), pick(code_b, 1, step, KEY)], axis=0
             )
@@ -337,11 +373,17 @@
                 heads_grad[r, lanes, :].astype(jnp.float32) * inverse
             ).astype(jnp.bfloat16)
 
+    for kind in (KEY, VALUE):
+        for way in (RIGHT, LEFT):
+            for hop in range(1, last_hop(way, kind) + 1):
+                for half in range(2):
+                    gather_hop(way, kind, half, hop).wait_send()
+
     def backward(dist, requests, first):
         slot = dist % 2
         found = []
         for r in requests:
-            code_a, code_b = table[0, r, dist], table[1, r, dist]
+            code_a, code_b = table[r, dist], table[r, AHEAD + dist]
             vals = jnp.concatenate(
                 [pick(code_a, 0, dist, VALUE), pick(code_b, 1, dist, VALUE)], axis=0
             )
@@ -444,6 +486,7 @@
     for j in range(1, M):
         total += dot(w_ref[:, j * depth : (j + 1) * depth], heads[j], NN)
     attn_ref[...] = total
+    attn_copy.start()
 
     for kind in (KEY, VALUE):
         for half in range(2):
@@ -458,8 +501,8 @@
         for way in (RIGHT, LEFT):
             for hop in range(1, last_hop(way, kind) + 1):
                 for half in range(2):
-                    gather_hop(way, kind, half, hop).wait_send()
                     ring_hop(way, kind, half, hop).wait_send()
+    attn_copy.wait()
     for i in range(1, X):
         q_copy(i).wait_send()
         g_copy(i).wait_send()
@@ -487,22 +530,9 @@
 ):
     M = lax.axis_size("mp")
     H = Z // 2
-    req = lax.axis_index("req")
-    z, x = req // X, req % X
     tokens, heads_width = queries.shape
     group = heads_width // HD
     width = out_weight.shape[1]
-    blk_dev = bank.shape[0] // BLOCK
-
-    lists = lax.dynamic_slice_in_dim(block_list, z * X, X, 0)
-    counts = lax.dynamic_slice_in_dim(block_count, z * X, X, 0)
-    steps = jnp.arange(H + 1, dtype=jnp.int32)
-    behind = ((z - steps) % Z) * X + x
-    ahead = jnp.where(steps == H, z, (z + steps) % Z) * X + x
-    owners = jnp.stack([behind, ahead])
-    used = lax.broadcasted_iota(jnp.int32, lists.shape, 1) < counts[:, None]
-    hit = used[None, :, None, :] & (lists[None, :, None, :] // blk_dev == owners[:, None, :, None])
-    table = jnp.sum(jnp.where(hit, 1 + lists[None, :, None, :] % blk_dev, 0), axis=-1)
 
     flat = (2 * bank.shape[0], HD)
     bf16, f32 = jnp.bfloat16, jnp.float32
@@ -511,15 +541,21 @@
     dma = pltpu.SemaphoreType.DMA
     smem_spec = pl.BlockSpec(memory_space=pltpu.SMEM)
     vmem_spec = pl.BlockSpec(memory_space=pltpu.VMEM)
+    any_spec = pl.BlockSpec(memory_space=pl.ANY)
     attn_out, grad = pl.pallas_call(
         functools.partial(step_kernel, (Z, X, M)),
         out_shape=(
             jax.ShapeDtypeStruct((width, tokens), f32),
             jax.ShapeDtypeStruct(flat, f32),
         ),
-        in_specs=[smem_spec, smem_spec] + [vmem_spec] * 6,
-        out_specs=(vmem_spec, vmem_spec),
+        in_specs=[smem_spec, smem_spec] + [vmem_spec] * 5 + [any_spec] * 2,
+        out_specs=(any_spec, vmem_spec),
         scratch_shapes=[
+            vmem((width, out_weight.shape[0]), bf16),
+            vmem((width, tokens), bf16),
+            vmem((width, tokens), f32),
+            vmem((X, HD), jnp.int32),
+            pltpu.SMEM((X, HD), jnp.int32),
             vmem((2, H + 1, 2, rows_local, HD), bf16),
             vmem((X, tokens, heads_width), bf16),
             vmem((X, heads_width, tokens), bf16),
@@ -555,14 +591,15 @@
             dma((M,)),
             dma((M,)),
             dma((2, H + 1, 4)),
-            dma((2, H + 1, 4)),
+            dma((4,)),
         ],
         compiler_params=pltpu.CompilerParams(
             collective_id=0, has_side_effects=True, vmem_limit_bytes=56 << 20
         ),
     )(
-        table,
+        block_count,
         token_count,
+        block_list.T,
         bank.reshape(flat),
         queries,
         keys,
@@ -571,7 +608,9 @@
         out_grad.T,
     )
 
-    one, two = moment_one.reshape(flat), moment_two.reshape(flat)
+    grad, bank, one, two = lax.optimization_barrier(
+        (grad, bank, moment_one.reshape(flat), moment_two.reshape(flat))
+    )
     moment_next = beta_one * one + (1.0 - beta_one) * grad
     second_next = beta_two * two + (1.0 - beta_two) * grad * grad
     bank_next = bank.reshape(flat) - learn_rate * (moment_next / bias_one) / (

time: 96.1 us -> 90.7 us (0.944)
  other arithmetic: 4.64 us -> 1.92 us
  local copies, waits for them, and re-layouts: 3.51 us -> 1.93 us
  Pallas kernels: 85 us -> 83.8 us
    mul x2 -> x0, other arithmetic: 2.17 us -> none  [the longest x1 1.09 us: local(): second_next = beta_two * two + (1.0 - beta_two) * grad * grad]
    pallas_call x1, Pallas kernels: 85 us -> 83.8 us  [local(): pl.pallas_call(functools.partial(step_kernel, (Z, X, M)), out_shape=(jax....]
    unnamed x6 -> x7, local copies, waits for them, and re-layouts: 2.01 us -> 1.93 us
where the time goes in v3:
time: 90.7 us; the launch traced here: 89 us
  Pallas kernels  83.8 us (92%)
  local copies, waits for them, and re-layouts  1.93 us (2%)
  other arithmetic  1.92 us (2%)
  between operations  1.41 us (2%)
    pallas_call x1, Pallas kernels, local(): pl.pallas_call(functools.partial(step_kernel, (Z, X, M)), out_shape=(jax....  83.8 us
    unnamed x7, local copies, waits for them, and re-layouts  1.93 us
    sub x1, other arithmetic, local(): bank.reshape(flat)  1.92 us

profile of v3, /device:TPU:24, one launch (start us, length us, event | category | flops | bytes accessed | tf_op | source)
XLA Modules:
  0.0 89.0 jit_solution(8741871801625577751)
XLA Ops:
  0.6 0.0 copy-start
  0.6 0.0 copy-start.2
  0.7 0.0 copy-start.1
  1.4 83.8 %shard_map.138 = (f32[576,256]{1,0:T(8,128)}, f32[512,128]{1,0:T(8,128)}) custom-call(s32[64]{0:T(128)} %block_count.1, s32[1]{0:T(128)S(6)} %copy.16.token_count, s32[32,64]{1,0:T(8,128)} %bitcast.21, f32[512,128]{1,0:T(8,128)} %bitcast.12, bf16[256,256]{1,0:T(8,128)(2,1)} %q_ref.1, bf16[256,128]{1,0:T(8,128)(2,1)} %k_ref.1, bf16[256,128]{1,0:T(8,128)(2,1)} %v_ref.1, ...), custom_call_target="tpu_custom_call" | custom-call | tf_op jit(solution)/shard_map/pallas_call | solution.py:545
  85.2 0.0 copy-done
  85.2 0.0 copy-done.2
  85.2 0.0 copy-done.1
  85.2 1.9 %divide_subtract_fusion = (f32[512,128]{1,0:T(8,128)}, f32[512,128]{1,0:T(8,128)}, f32[512,128]{1,0:T(8,128)}) fusion(f32[512,128]{1,0:T(8,128)S(1)} %bitcast.13, f32[512,128]{1,0:T(8,128)} %get-tuple-element.14, f32[512,128]{1,0:T(8,128)S(1)} %bitcast.16, f32[512,128]{1,0:T(8,128)S(1)} %bitcast.17), kind=kLoop, calls=%fused_computation.2 | loop fusion | flops 786432 | bytes 1835008 | tf_op jit(solution)/shard_map/sub | solution.py:616
  87.1 1.9 %copy.17 = f32[256,576]{0,1:T(8,128)} copy(f32[256,576]{0,1:T(8,128)} %bitcast.14) | data formatting | bytes 1179648
Async XLA Ops:
  0.6 84.6 %copy-start = (f32[256,2,128]{2,1,0:T(2,128)S(1)}, f32[256,2,128]{2,1,0:T(2,128)}, u32[]{:S(2)}) copy-start(f32[256,2,128]{2,1,0:T(2,128)} %param.16) | copy-start | bytes 786436
  0.6 84.6 %copy-start.2 = (f32[256,2,128]{2,1,0:T(2,128)S(1)}, f32[256,2,128]{2,1,0:T(2,128)}, u32[]{:S(2)}) copy-start(f32[256,2,128]{2,1,0:T(2,128)} %param.18) | copy-start | bytes 786436
  0.7 84.6 %copy-start.1 = (f32[256,2,128]{2,1,0:T(2,128)S(1)}, f32[256,2,128]{2,1,0:T(2,128)}, u32[]{:S(2)}) copy-start(f32[256,2,128]{2,1,0:T(2,128)} %param.17) | copy-start | bytes 786436

commit v4 on v3

--- a/solution.py
+++ b/solution.py
@@ -73,7 +73,7 @@
     own_sum,
     ring_send,
     ring_recv,
-    ag_send_sem,
+    ring_send_sem,
     ag_recv_sem,
     q_send_sem,
     q_recv_sem,
@@ -124,7 +124,7 @@
         return remote(
             slab.at[way, hop - 1, kind, span],
             slab.at[lane, hop, kind, span],
-            ag_send_sem.at[way, hop, 2 * kind + half],
+            ring_send_sem.at[way, hop % 2, 2 * kind + half],
             ag_recv_sem.at[way, hop, 2 * kind + half],
             toward[way],
         )
@@ -163,7 +163,7 @@
         return remote(
             ring_send.at[way, dist, kind, span],
             ring_recv.at[way, dist - 1, kind, span],
-            ag_send_sem.at[way, dist, 2 * kind + half],
+            ring_send_sem.at[way, dist % 2, 2 * kind + half],
             rs_recv_sem.at[way, dist, 2 * kind + half],
             toward[way],
         )
@@ -294,6 +294,10 @@
                 def _():
                     gather_hop(way, kind, half, step).wait_recv()
 
+                @pl.when((step < last) & (step > 1))
+                def _():
+                    gather_hop(way, kind, half, step - 1).wait_send()
+
                 @pl.when(step < last)
                 def _():
                     gather_hop(way, kind, half, step + 1).start()
@@ -358,6 +362,17 @@
         n_copy(i).start()
     ring_recv[RIGHT, H - 1, VALUE] = jnp.zeros_like(ring_recv[RIGHT, H - 1, VALUE])
     ring_recv[LEFT, H - 1, KEY] = jnp.zeros_like(ring_recv[LEFT, H - 1, KEY])
+    for kind in (KEY, VALUE):
+        for way in (RIGHT, LEFT):
+            last = last_hop(way, kind)
+            for hop in range(max(1, last - 1), last + 1):
+                for half in range(2):
+                    gather_hop(way, kind, half, hop).wait_send()
+    for i in range(1, X):
+        q_copy(i).wait_send()
+        g_copy(i).wait_send()
+    for i in range(1, M):
+        h_copy(i).wait_send()
     stats = stat_send[...]
     for i in range(1, X):
         s_copy(i).wait_recv()
@@ -372,12 +387,6 @@
             scaled_grad[r, lanes, :] = (
                 heads_grad[r, lanes, :].astype(jnp.float32) * inverse
             ).astype(jnp.bfloat16)
-
-    for kind in (KEY, VALUE):
-        for way in (RIGHT, LEFT):
-            for hop in range(1, last_hop(way, kind) + 1):
-                for half in range(2):
-                    gather_hop(way, kind, half, hop).wait_send()
 
     def backward(dist, requests, first):
         slot = dist % 2
@@ -436,6 +445,11 @@
                         part[slot, side, kind, span, :]
                         + ring_recv[way, dist, kind, span, :].astype(jnp.float32)
                     ).astype(jnp.bfloat16)
+
+                    @pl.when(dist + 2 <= last)
+                    def _():
+                        ring_hop(way, kind, half, dist + 2).wait_send()
+
                     ring_hop(way, kind, half, dist).start()
 
     def scatter_step(index, carry):
@@ -487,6 +501,11 @@
         total += dot(w_ref[:, j * depth : (j + 1) * depth], heads[j], NN)
     attn_ref[...] = total
     attn_copy.start()
+    for i in range(1, X):
+        s_copy(i).wait_send()
+        n_copy(i).wait_send()
+    for i in range(1, M):
+        a_copy(i).wait_send()
 
     for kind in (KEY, VALUE):
         for half in range(2):
@@ -499,18 +518,44 @@
 
     for kind in (KEY, VALUE):
         for way in (RIGHT, LEFT):
-            for hop in range(1, last_hop(way, kind) + 1):
+            for dist in range(1, min(2, last_hop(way, kind)) + 1):
                 for half in range(2):
-                    ring_hop(way, kind, half, hop).wait_send()
+                    ring_hop(way, kind, half, dist).wait_send()
     attn_copy.wait()
-    for i in range(1, X):
-        q_copy(i).wait_send()
-        g_copy(i).wait_send()
-        s_copy(i).wait_send()
-        n_copy(i).wait_send()
-    for i in range(1, M):
-        h_copy(i).wait_send()
-        a_copy(i).wait_send()
+
+
+def update_kernel(
+    grad_ref,
+    bank_ref,
+    one_ref,
+    two_ref,
+    attn_ref,
+    attn_out,
+    bank_out,
+    one_out,
+    two_out,
+    sems,
+):
+    pieces = sems.shape[0]
+    size = attn_ref.shape[0] // pieces
+    copies = [
+        pltpu.make_async_copy(
+            attn_ref.at[pl.ds(i * size, size)], attn_out.at[pl.ds(i * size, size)], sems.at[i]
+        )
+        for i in range(pieces)
+    ]
+    for copy in copies:
+        copy.start()
+    grad = grad_ref[...]
+    moment_next = beta_one * one_ref[...] + (1.0 - beta_one) * grad
+    second_next = beta_two * two_ref[...] + (1.0 - beta_two) * grad * grad
+    one_out[...] = moment_next
+    two_out[...] = second_next
+    bank_out[...] = bank_ref[...] - learn_rate * (moment_next / bias_one) / (
+        jnp.sqrt(second_next / bias_two) + adam_eps
+    )
+    for copy in copies:
+        copy.wait()
 
 
 def local(
@@ -576,7 +621,7 @@
             vmem((2, rows_local, HD), f32),
             vmem((2, H + 1, 2, rows_local, HD), bf16),
             vmem((2, H + 1, 2, rows_local, HD), bf16),
-            dma((2, H + 1, 4)),
+            dma((2, 2, 4)),
             dma((2, H + 1, 4)),
             dma((X,)),
             dma((X,)),
@@ -608,14 +653,14 @@
         out_grad.T,
     )
 
-    grad, bank, one, two = lax.optimization_barrier(
-        (grad, bank, moment_one.reshape(flat), moment_two.reshape(flat))
-    )
-    moment_next = beta_one * one + (1.0 - beta_one) * grad
-    second_next = beta_two * two + (1.0 - beta_two) * grad * grad
-    bank_next = bank.reshape(flat) - learn_rate * (moment_next / bias_one) / (
-        jnp.sqrt(second_next / bias_two) + adam_eps
-    )
+    attn_out, bank_next, moment_next, second_next = pl.pallas_call(
+        update_kernel,
+        out_shape=(jax.ShapeDtypeStruct((width, tokens), f32),)
+        + (jax.ShapeDtypeStruct(flat, f32),) * 3,
+        in_specs=[vmem_spec] * 4 + [any_spec],
+        out_specs=(any_spec,) + (vmem_spec,) * 3,
+        scratch_shapes=[dma((4,))],
+    )(grad, bank.reshape(flat), moment_one.reshape(flat), moment_two.reshape(flat), attn_out)
     return (
         attn_out.T,
         bank_next.reshape(bank.shape),

time: 90.7 us -> 107 us (1.18)
  Pallas kernels: 83.8 us -> 104 us
  local copies, waits for them, and re-layouts: 1.93 us -> 0 us
  other arithmetic: 1.92 us -> 0 us
    pallas_call x0 -> x1, Pallas kernels: none -> 21.1 us  [local(): pl.pallas_call(update_kernel, out_shape=(jax.ShapeDtypeStruct((width, tok...]
    unnamed x7 -> x0, local copies, waits for them, and re-layouts: 1.93 us -> none
    sub x1 -> x0, other arithmetic: 1.92 us -> none  [local(): bank.reshape(flat)]
where the time goes in v4:
time: 107 us; the launch traced here: 106 us
  Pallas kernels  104 us (97%)
  between operations  1.29 us (1%)
    pallas_call x1, Pallas kernels, local(): pl.pallas_call(functools.partial(step_kernel, (Z, X, M)), out_shape=(jax....  83.4 us
    pallas_call x1, Pallas kernels, local(): pl.pallas_call(update_kernel, out_shape=(jax.ShapeDtypeStruct((width, tok...  21.1 us

profile of v4, /device:TPU:24, one launch (start us, length us, event | category | flops | bytes accessed | tf_op | source)
XLA Modules:
  0.0 105.7 jit_solution(6231449397774723363)
XLA Ops:
  1.3 83.4 %shard_map.138 = (f32[576,256]{1,0:T(8,128)}, f32[512,128]{1,0:T(8,128)}) custom-call(s32[64]{0:T(128)} %block_count.1, s32[1]{0:T(128)S(6)} %copy.15.token_count, s32[32,64]{1,0:T(8,128)} %bitcast.16, f32[512,128]{1,0:T(8,128)} %bitcast.11, bf16[256,256]{1,0:T(8,128)(2,1)} %q_ref.1, bf16[256,128]{1,0:T(8,128)(2,1)} %k_ref.1, bf16[256,128]{1,0:T(8,128)(2,1)} %v_ref.1, ...), custom_call_target="tpu_custom_call" | custom-call | tf_op jit(solution)/shard_map/pallas_call | solution.py:590
  84.6 21.1 %shard_map.139 = (f32[576,256]{1,0:T(8,128)}, f32[512,128]{1,0:T(8,128)}, f32[512,128]{1,0:T(8,128)}, f32[512,128]{1,0:T(8,128)}) custom-call(f32[512,128]{1,0:T(8,128)} %get-tuple-element.10.grad_ref, f32[512,128]{1,0:T(8,128)} %bitcast.12, f32[512,128]{1,0:T(8,128)} %bitcast.14, f32[512,128]{1,0:T(8,128)} %bitcast.15, f32[576,256]{1,0:T(8,128)} %get-tuple-element.11.attn_ref), custom_call_target="tpu_custom_call" | custom-call | tf_op jit(solution)/shard_map/pallas_call | solution.py:656

commit v5 on v4

--- a/solution.py
+++ b/solution.py
@@ -534,18 +534,8 @@
     bank_out,
     one_out,
     two_out,
-    sems,
 ):
-    pieces = sems.shape[0]
-    size = attn_ref.shape[0] // pieces
-    copies = [
-        pltpu.make_async_copy(
-            attn_ref.at[pl.ds(i * size, size)], attn_out.at[pl.ds(i * size, size)], sems.at[i]
-        )
-        for i in range(pieces)
-    ]
-    for copy in copies:
-        copy.start()
+    attn_out[...] = attn_ref[...]
     grad = grad_ref[...]
     moment_next = beta_one * one_ref[...] + (1.0 - beta_one) * grad
     second_next = beta_two * two_ref[...] + (1.0 - beta_two) * grad * grad
@@ -554,8 +544,6 @@
     bank_out[...] = bank_ref[...] - learn_rate * (moment_next / bias_one) / (
         jnp.sqrt(second_next / bias_two) + adam_eps
     )
-    for copy in copies:
-        copy.wait()
 
 
 def local(
@@ -653,13 +641,17 @@
         out_grad.T,
     )
 
+
+    def half_rows(rows, columns):
+        return pl.BlockSpec((rows // 2, columns), lambda i: (i, 0))
+
     attn_out, bank_next, moment_next, second_next = pl.pallas_call(
         update_kernel,
         out_shape=(jax.ShapeDtypeStruct((width, tokens), f32),)
         + (jax.ShapeDtypeStruct(flat, f32),) * 3,
-        in_specs=[vmem_spec] * 4 + [any_spec],
-        out_specs=(any_spec,) + (vmem_spec,) * 3,
-        scratch_shapes=[dma((4,))],
+        grid=(2,),
+        in_specs=[half_rows(*flat)] * 4 + [half_rows(width, tokens)],
+        out_specs=(half_rows(width, tokens),) + (half_rows(*flat),) * 3,
     )(grad, bank.reshape(flat), moment_one.reshape(flat), moment_two.reshape(flat), attn_out)
     return (
         attn_out.T,

time: 107 us -> 88.3 us (0.83)
  Pallas kernels: 104 us -> 85.8 us
    pallas_call x1, Pallas kernels: 21.1 us -> 2.41 us  [local(): pl.pallas_call(update_kernel, out_shape=(jax.ShapeDtypeStruct((width, tok...]
where the time goes in v5:
time: 88.3 us; the launch traced here: 87.1 us
  Pallas kernels  85.8 us (97%)
  between operations  1.29 us (1%)
    pallas_call x1, Pallas kernels, local(): pl.pallas_call(functools.partial(step_kernel, (Z, X, M)), out_shape=(jax....  83.4 us
    pallas_call x1, Pallas kernels, local(): pl.pallas_call(update_kernel, out_shape=(jax.ShapeDtypeStruct((width, tok...  2.41 us

profile of v5, /device:TPU:24, one launch (start us, length us, event | category | flops | bytes accessed | tf_op | source)
XLA Modules:
  0.0 87.1 jit_solution(4964916175396932580)
XLA Ops:
  1.3 83.4 %shard_map.138 = (f32[576,256]{1,0:T(8,128)}, f32[512,128]{1,0:T(8,128)}) custom-call(s32[64]{0:T(128)} %block_count.1, s32[1]{0:T(128)S(6)} %copy.15.token_count, s32[32,64]{1,0:T(8,128)} %bitcast.16, f32[512,128]{1,0:T(8,128)} %bitcast.11, bf16[256,256]{1,0:T(8,128)(2,1)} %q_ref.1, bf16[256,128]{1,0:T(8,128)(2,1)} %k_ref.1, bf16[256,128]{1,0:T(8,128)(2,1)} %v_ref.1, ...), custom_call_target="tpu_custom_call" | custom-call | tf_op jit(solution)/shard_map/pallas_call | solution.py:578
  84.6 2.4 %shard_map.139 = (f32[576,256]{1,0:T(8,128)}, f32[512,128]{1,0:T(8,128)}, f32[512,128]{1,0:T(8,128)}, f32[512,128]{1,0:T(8,128)}) custom-call(f32[512,128]{1,0:T(8,128)} %get-tuple-element.10.grad_ref, f32[512,128]{1,0:T(8,128)} %bitcast.12, f32[512,128]{1,0:T(8,128)} %bitcast.14, f32[512,128]{1,0:T(8,128)} %bitcast.15, f32[576,256]{1,0:T(8,128)} %get-tuple-element.11.attn_ref), custom_call_target="tpu_custom_call" | custom-call | tf_op jit(solution)/shard_map/pallas_call | solution.py:648

commit v6 on v5

--- a/solution.py
+++ b/solution.py
@@ -71,6 +71,7 @@
     heads,
     part,
     own_sum,
+    first_prob,
     ring_send,
     ring_recv,
     ring_send_sem,
@@ -251,17 +252,18 @@
             code == 2, slab[way, step, kind, BLOCK:, :], slab[way, step, kind, :BLOCK, :]
         )
 
-    def forward(step, offsets):
+    def join(pieces):
+        return pieces[0] if len(pieces) == 1 else jnp.concatenate(pieces, axis=0)
+
+    def forward(step, offsets, sides=(0, 1)):
+        covered = slice(sides[0] * BLOCK, (sides[-1] + 1) * BLOCK)
         for offset in offsets:
             r = (x + offset) % X
-            code_a, code_b = table[r, step], table[r, AHEAD + step]
-            keys = jnp.concatenate(
-                [pick(code_a, 0, step, KEY), pick(code_b, 1, step, KEY)], axis=0
-            )
-            val_a, val_b = pick(code_a, 0, step, VALUE), pick(code_b, 1, step, VALUE)
-            zero = jnp.zeros_like(val_a)
-            vals = jnp.concatenate(
-                [choose(code_a > 0, val_a, zero), choose(code_b > 0, val_b, zero)], axis=0
+            taken = [table[r, side * AHEAD + step] for side in sides]
+            keys = join([pick(code, side, step, KEY) for side, code in zip(sides, taken)])
+            chosen = [pick(code, side, step, VALUE) for side, code in zip(sides, taken)]
+            vals = join(
+                [choose(code > 0, val, jnp.zeros_like(val)) for val, code in zip(chosen, taken)]
             )
             halves = []
             for g in range(group):
@@ -270,14 +272,15 @@
                 exp = jnp.exp(softcap * tanh)
                 half = exp.astype(jnp.bfloat16)
                 halves.append(half)
-                exps[step - 1, r, g] = half
-                slopes[step - 1, r, g] = (exp * (1.0 - tanh * tanh)).astype(jnp.bfloat16)
-                sum_a = jnp.sum(exp[:BLOCK], axis=0, keepdims=True)
-                sum_b = jnp.sum(exp[BLOCK:], axis=0, keepdims=True)
-                none = jnp.zeros_like(sum_a)
-                denom[r, g : g + 1, :] += choose(code_a > 0, sum_a, none) + choose(
-                    code_b > 0, sum_b, none
+                exps[step - 1, r, g, covered, :] = half
+                slopes[step - 1, r, g, covered, :] = (exp * (1.0 - tanh * tanh)).astype(
+                    jnp.bfloat16
                 )
+                added = denom[r, g : g + 1, :]
+                for i, code in enumerate(taken):
+                    mine = jnp.sum(exp[i * BLOCK : (i + 1) * BLOCK], axis=0, keepdims=True)
+                    added += choose(code > 0, mine, jnp.zeros_like(mine))
+                denom[r, g : g + 1, :] = added
             mixed = dot(vals, jnp.concatenate(halves, axis=1), TN)
             for g in range(group):
                 numer[r, g * HD : (g + 1) * HD, :] += mixed[:, g * tokens : (g + 1) * tokens]
@@ -312,9 +315,13 @@
             for i in late:
                 q_copy(X - i).wait_recv()
 
-        @pl.when(step > 1)
+        @pl.when((step > 1) & (step <= H))
         def _():
             forward(step - 1, late)
+
+        @pl.when(step == H + 1)
+        def _():
+            forward(H, late, (0,))
 
         @pl.when(step <= H)
         def _():
@@ -325,9 +332,21 @@
             for i in early[1:]:
                 q_copy(X - i).wait_recv()
 
-        @pl.when(step <= H)
+        @pl.when(step < H)
         def _():
             forward(step, early)
+
+        @pl.when(step == H)
+        def _():
+            forward(H, early, (0,))
+
+        @pl.when(step == max(2, H // 2 - 1))
+        def _():
+            forward(H, early, (1,))
+
+        @pl.when(step == max(2, H // 2))
+        def _():
+            forward(H, late, (1,))
 
         @pl.when(step == min(6, H))
         def _():
@@ -373,6 +392,10 @@
         g_copy(i).wait_send()
     for i in range(1, M):
         h_copy(i).wait_send()
+    for r in range(X):
+        vals = join([pick(table[r, side * AHEAD + H], side, H, VALUE) for side in range(2)])
+        for g in range(group):
+            first_prob[r, g] = dot(vals, heads_grad[r, g * HD : (g + 1) * HD, :], NN)
     stats = stat_send[...]
     for i in range(1, X):
         s_copy(i).wait_recv()
@@ -388,21 +411,24 @@
                 heads_grad[r, lanes, :].astype(jnp.float32) * inverse
             ).astype(jnp.bfloat16)
 
-    def backward(dist, requests, first):
+    def backward(dist, requests, first, known=False):
         slot = dist % 2
         found = []
         for r in requests:
             code_a, code_b = table[r, dist], table[r, AHEAD + dist]
-            vals = jnp.concatenate(
-                [pick(code_a, 0, dist, VALUE), pick(code_b, 1, dist, VALUE)], axis=0
-            )
+            vals = None
+            if not known:
+                vals = join([pick(code_a, 0, dist, VALUE), pick(code_b, 1, dist, VALUE)])
             key_grad = jnp.zeros((2 * BLOCK, HD), jnp.float32)
             value_grad = jnp.zeros((2 * BLOCK, HD), jnp.float32)
             for g in range(group):
                 lanes = slice(g * HD, (g + 1) * HD)
                 inverse = rows[r, 2 * g : 2 * g + 1, :]
                 delta = rows[r, 2 * g + 1 : 2 * g + 2, :]
-                dprob = dot(vals, heads_grad[r, lanes, :], NN)
+                if known:
+                    dprob = first_prob[r, g]
+                else:
+                    dprob = dot(vals, heads_grad[r, lanes, :], NN)
                 slope = slopes[dist - 1, r, g].astype(jnp.float32)
                 dscore = slope * ((dprob - delta) * (inverse * qscale))
                 key_grad += dot(dscore.astype(jnp.bfloat16), queries[r, :, lanes], NN)
@@ -455,25 +481,17 @@
     def scatter_step(index, carry):
         dist = H + 1 - index
 
-        @pl.when(dist <= H)
-        def _():
-            hand_over(dist, KEY)
+        hand_over(dist, KEY)
 
         @pl.when(dist > 1)
         def _():
             backward(dist - 1, range(X // 2), True)
 
-        @pl.when(dist <= H)
-        def _():
-            hand_over(dist, VALUE)
+        hand_over(dist, VALUE)
 
         @pl.when(dist > 1)
         def _():
             backward(dist - 1, range(X // 2, X), False)
-
-        @pl.when(index == 0)
-        def _():
-            own_sum[...] = part[H % 2, 1]
 
         @pl.when(index == min(4, H))
         def _():
@@ -491,7 +509,9 @@
 
         return carry
 
-    lax.fori_loop(0, H + 1, scatter_step, 0)
+    backward(H, range(X), True, known=True)
+    own_sum[...] = part[H % 2, 1]
+    lax.fori_loop(1, H + 1, scatter_step, 0)
 
     for i in range(1, M):
         a_copy(i).wait_recv()
@@ -607,6 +627,7 @@
             vmem((M, heads_width, tokens), bf16),
             vmem((2, 2, 2, rows_local, HD), f32),
             vmem((2, rows_local, HD), f32),
+            vmem((X, group, 2 * BLOCK, tokens), f32),
             vmem((2, H + 1, 2, rows_local, HD), bf16),
             vmem((2, H + 1, 2, rows_local, HD), bf16),
             dma((2, 2, 4)),

time: 88.3 us -> 87.8 us (level)
  no operation moved by 1% of the time
where the time goes in v6:
time: 87.8 us; the launch traced here: 86.8 us
  Pallas kernels  85.5 us (97%)
  between operations  1.29 us (1%)
    pallas_call x1, Pallas kernels, local(): pl.pallas_call(functools.partial(step_kernel, (Z, X, M)), out_shape=(jax....  83.1 us
    pallas_call x1, Pallas kernels, local(): pl.pallas_call(update_kernel, out_shape=(jax.ShapeDtypeStruct((width, tok...  2.41 us

profile of v6, /device:TPU:24, one launch (start us, length us, event | category | flops | bytes accessed | tf_op | source)
XLA Modules:
  0.0 86.8 jit_solution(15314899481732306257)
XLA Ops:
  1.3 83.1 %shard_map.138 = (f32[576,256]{1,0:T(8,128)}, f32[512,128]{1,0:T(8,128)}) custom-call(s32[64]{0:T(128)} %block_count.1, s32[1]{0:T(128)S(6)} %copy.15.token_count, s32[32,64]{1,0:T(8,128)} %bitcast.16, f32[512,128]{1,0:T(8,128)} %bitcast.11, bf16[256,256]{1,0:T(8,128)(2,1)} %q_ref.1, bf16[256,128]{1,0:T(8,128)(2,1)} %k_ref.1, bf16[256,128]{1,0:T(8,128)(2,1)} %v_ref.1, ...), custom_call_target="tpu_custom_call" | custom-call | tf_op jit(solution)/shard_map/pallas_call | solution.py:598
  84.4 2.4 %shard_map.139 = (f32[576,256]{1,0:T(8,128)}, f32[512,128]{1,0:T(8,128)}, f32[512,128]{1,0:T(8,128)}, f32[512,128]{1,0:T(8,128)}) custom-call(f32[512,128]{1,0:T(8,128)} %get-tuple-element.10.grad_ref, f32[512,128]{1,0:T(8,128)} %bitcast.12, f32[512,128]{1,0:T(8,128)} %bitcast.14, f32[512,128]{1,0:T(8,128)} %bitcast.15, f32[576,256]{1,0:T(8,128)} %get-tuple-element.11.attn_ref), custom_call_target="tpu_custom_call" | custom-call | tf_op jit(solution)/shard_map/pallas_call | solution.py:669

commit v7 on v6

--- a/solution.py
+++ b/solution.py
@@ -348,7 +348,7 @@
         def _():
             forward(H, late, (1,))
 
-        @pl.when(step == min(6, H))
+        @pl.when(step == min(5, H))
         def _():
             total = hg_send[0].astype(jnp.float32)
             for i in range(1, M):

time: 87.8 us -> 87.6 us (level)
  no operation moved by 1% of the time
where the time goes in v7:
time: 87.6 us; the launch traced here: 86.5 us
  Pallas kernels  85.2 us (97%)
  between operations  1.29 us (1%)
    pallas_call x1, Pallas kernels, local(): pl.pallas_call(functools.partial(step_kernel, (Z, X, M)), out_shape=(jax....  82.8 us
    pallas_call x1, Pallas kernels, local(): pl.pallas_call(update_kernel, out_shape=(jax.ShapeDtypeStruct((width, tok...  2.41 us

profile of v7, /device:TPU:24, one launch (start us, length us, event | category | flops | bytes accessed | tf_op | source)
XLA Modules:
  0.0 86.5 jit_solution(1869426774648124986)
XLA Ops:
  1.3 82.8 %shard_map.138 = (f32[576,256]{1,0:T(8,128)}, f32[512,128]{1,0:T(8,128)}) custom-call(s32[64]{0:T(128)} %block_count.1, s32[1]{0:T(128)S(6)} %copy.15.token_count, s32[32,64]{1,0:T(8,128)} %bitcast.16, f32[512,128]{1,0:T(8,128)} %bitcast.11, bf16[256,256]{1,0:T(8,128)(2,1)} %q_ref.1, bf16[256,128]{1,0:T(8,128)(2,1)} %k_ref.1, bf16[256,128]{1,0:T(8,128)(2,1)} %v_ref.1, ...), custom_call_target="tpu_custom_call" | custom-call | tf_op jit(solution)/shard_map/pallas_call | solution.py:598
  84.1 2.4 %shard_map.139 = (f32[576,256]{1,0:T(8,128)}, f32[512,128]{1,0:T(8,128)}, f32[512,128]{1,0:T(8,128)}, f32[512,128]{1,0:T(8,128)}) custom-call(f32[512,128]{1,0:T(8,128)} %get-tuple-element.10.grad_ref, f32[512,128]{1,0:T(8,128)} %bitcast.12, f32[512,128]{1,0:T(8,128)} %bitcast.14, f32[512,128]{1,0:T(8,128)} %bitcast.15, f32[576,256]{1,0:T(8,128)} %get-tuple-element.11.attn_ref), custom_call_target="tpu_custom_call" | custom-call | tf_op jit(solution)/shard_map/pallas_call | solution.py:669
